TPU v7x, 32 devices: a whole 2x2x4 slice. The times are simulated.
32 devices in a mesh: grp: 2 (over y), loan: 4 (over z), feat: 4 (over x, core).
Axes of the slice: x: 2, y: 2, z: 4, core: 2. Of those that a mesh axis runs over, the one named last changes fastest.
Arguments:
- design: bfloat16 [16384, 4096], P(('grp', 'loan'), 'feat'), parts along dimension 0, may hold values from -6 to 6
- labels: int32 [16384], P(('grp', 'loan')), parts along dimension 0, may hold values from 0 to 1
- pool_ids: int32 [16384], P(('grp', 'loan')), parts along dimension 0, may hold values from 0 to 255, as said below
- pool_region_index: int32 [512], P(('grp', 'loan')), parts along dimension 0, may hold values from 0 to 63
- step_size: float32 [32], P('grp'), parts along dimension 0, may hold values from 0.005 to 0.02
- beta: float32 [32, 4096], P('grp', 'feat'), parts along dimension 0, may hold values from -0.09375 to 0.09375
- pools: float32 [32, 256, 256], P('grp', 'loan', 'feat'), parts along dimension 0, may hold values from -0.5 to 0.5
- regions: float32 [32, 64, 256], P('grp', None, 'feat'), parts along dimension 0, may hold values from -0.5 to 0.5
- beta_momentum: float32 [32, 4096], P('grp', 'feat'), parts along dimension 0, may hold values from -6 to 6
- pool_momentum: float32 [32, 256, 256], P('grp', 'loan', 'feat'), parts along dimension 0, may hold values from -6 to 6
- region_momentum: float32 [32, 64, 256], P('grp', None, 'feat'), parts along dimension 0, may hold values from -6 to 6
Outputs:
- beta_next: float32 [32, 4096], P('grp', 'feat'), parts along dimension 0
- pools_next: float32 [32, 256, 256], P('grp', 'loan', 'feat'), parts along dimension 0
- regions_next: float32 [32, 64, 256], P('grp', None, 'feat'), parts along dimension 0
- beta_momentum_next: float32 [32, 4096], P('grp', 'feat'), parts along dimension 0
- pool_momentum_next: float32 [32, 256, 256], P('grp', 'loan', 'feat'), parts along dimension 0
- region_momentum_next: float32 [32, 64, 256], P('grp', None, 'feat'), parts along dimension 0
There are 2 independent parts, one for each index of `grp`. A program takes and returns all parts, laid end to end along the dimension named above; each array names one. Nothing has to cross between parts.
Inputs may be any that keep to these rules, and one draw needn't show every extreme that they name: `pool_ids`: in each aligned block of 2048 loans (block l counted from 0) the pool ids lie in l * 64 to (l + 1) * 64 - 1 and do not fall along the block.
All inputs are finite; a program needn't handle non-finite values.
Results may differ from a plain program's by a relative error of at most 0.0006.
Values may be sent and summed in bfloat16 or wider, within the bound.
A program may use at most 64 MiB of HBM per device.

v0:
```python
import functools

import jax
import jax.numpy as jnp
from jax import lax
from jax.experimental import pallas as pl
from jax.experimental.pallas import tpu as pltpu
from jax.sharding import PartitionSpec as P

PREC = 256.0
MESH = pl.DeviceIdType.MESH
NT = (((1,), (1,)), ((), ()))
NN = (((1,), (0,)), ((), ()))
F32 = jnp.float32
BF16 = jnp.bfloat16


def dot(a, b, dims=NN):
    return lax.dot_general(a, b, dims, preferred_element_type=F32)


def split3(x):
    hi = x.astype(BF16)
    rest = x - hi.astype(F32)
    mid = rest.astype(BF16)
    lo = (rest - mid.astype(F32)).astype(BF16)
    return jnp.concatenate([hi, mid, lo], axis=0)


def kernel(
    nf,
    nl,
    design_hbm,
    labels,
    ids,
    pri_row,
    step_s,
    beta,
    pools,
    regions,
    beta_m,
    pool_m,
    region_m,
    beta_n,
    pools_n,
    regions_n,
    beta_mn,
    pool_mn,
    region_mn,
    design,
    mask,
    slope_t,
    slope,
    u2,
    dev,
    lik,
    term,
    part,
    rs_buf,
    resid,
    resid_f,
    xt_buf,
    reg_part,
    reg_buf,
    reg_own,
    reg_all,
    load,
    s_rs,
    r_rs,
    s_ag,
    r_ag,
    s_xt,
    r_xt,
    s_rr,
    r_rr,
    s_ra,
    r_ra,
):
    fi = lax.axis_index("feat")
    li = lax.axis_index("loan")
    chains = beta.shape[0]
    feats = design.shape[1]
    owned = pools.shape[1]
    g_own = pools.shape[2]
    n_reg = regions.shape[1]
    width = labels.shape[2]
    per = chains // nl
    stride = feats // g_own
    total_feats = float(feats * nf)

    def at(axis, n, i, k):
        return lax.rem(i + k, n)

    fetch = pltpu.make_async_copy(design_hbm, design, load)
    fetch.start()
    fold = folds(n_reg, g_own)
    lines = n_reg // fold

    def pack(x):
        return jnp.concatenate([x[i * lines : (i + 1) * lines] for i in range(fold)], axis=1)

    def unpack(x):
        return jnp.concatenate([x[:, i * g_own : (i + 1) * g_own] for i in range(fold)], axis=0)

    barrier = pltpu.get_barrier_semaphore()
    for k in range(1, nf):
        pl.semaphore_signal(
            barrier, inc=1, device_id={"feat": at("feat", nf, fi, k)}, device_id_type=MESH
        )
    for k in range(1, nl):
        pl.semaphore_signal(
            barrier, inc=1, device_id={"loan": at("loan", nl, li, k)}, device_id_type=MESH
        )

    def rows(j):
        return design[pl.ds(pl.multiple_of(j * width, width), width), :]

    def remote(src, dst, ss, rs, axis, peer):
        return pltpu.make_async_remote_copy(
            src_ref=src,
            dst_ref=dst,
            send_sem=ss,
            recv_sem=rs,
            device_id={axis: peer},
            device_id_type=MESH,
        )

    def rs_copy(t, k):
        peer = lax.rem(fi + k, nf)
        return remote(
            part.at[t, peer], rs_buf.at[t, k - 1], s_rs.at[t, k - 1], r_rs.at[t, k - 1], "feat", peer
        )

    def ag_copy(t, k, slot):
        peer = lax.rem(fi + k, nf)
        return remote(
            resid.at[t, slot], resid.at[t, slot], s_ag.at[t, k - 1], r_ag.at[t, k - 1], "feat", peer
        )

    def xt_copy(t, k):
        peer = lax.rem(li + k, nl)
        return remote(
            xt_buf.at[t, 0], xt_buf.at[t, k], s_xt.at[t, k - 1], r_xt.at[t, k - 1], "loan", peer
        )

    def rr_copy(t, k):
        peer = lax.rem(li + k, nl)
        return remote(
            reg_part.at[t, pl.ds(peer * per, per)],
            reg_buf.at[t, k - 1],
            s_rr.at[t, k - 1],
            r_rr.at[t, k - 1],
            "loan",
            peer,
        )

    def ra_copy(t, k, owner):
        peer = lax.rem(li + k, nl)
        return remote(
            reg_own.at[t],
            reg_all.at[t, owner],
            s_ra.at[t, k - 1],
            r_ra.at[t, k - 1],
            "loan",
            peer,
        )

    oht = (pri_row[...] == lax.broadcasted_iota(jnp.int32, (n_reg, owned), 0)).astype(F32)
    eye = (
        lax.broadcasted_iota(jnp.int32, (owned, owned), 0)
        == lax.broadcasted_iota(jnp.int32, (owned, owned), 1)
    ).astype(F32)
    oh = dot(eye.astype(BF16), oht.astype(BF16), NT)
    oh3 = jnp.concatenate([oh, oh, oh], axis=1).astype(BF16)
    oht3 = jnp.concatenate([oht, oht, oht], axis=1).astype(BF16)

    def region_dev(t, u_ref, v_ref):
        for c in range(chains):
            d = PREC * (u_ref[c] - dot(oh3, split3(v_ref[c])))
            dev[c] = d
            reg_part[t, c] = pack(dot(oht3, split3(d)))
        for k in range(1, nl):
            rr_copy(t, k).start()

    def region_reduce(t):
        for k in range(1, nl):
            rr_copy(t, k).wait_recv()
        total = reg_part[t, pl.ds(li * per, per)]
        for k in range(1, nl):
            total = total + reg_buf[t, k - 1]
        reg_own[t] = total
        for k in range(1, nl):
            ra_copy(t, k, li).start()
        reg_all[t, li] = total

    def region_gather(t):
        for k in range(1, nl):
            ra_copy(t, k, lax.rem(li + nl - k, nl)).wait_recv()

    def pool_terms(u_ref):
        for c in range(chains):
            u = u_ref[c]
            hi = u.astype(BF16).astype(F32)
            both = jnp.concatenate([hi, u - hi], axis=1)
            u2[pl.ds(c * owned, owned), :] = both.astype(BF16)

        def chunk(j, carry):
            z = dot(u2[...], slope_t[j])
            m = mask[j]
            for c in range(chains):
                term[j, pl.ds(c, 1), :] = jnp.sum(
                    z[c * owned : (c + 1) * owned] * m, axis=0, keepdims=True
                )
            return carry

        lax.fori_loop(0, nf, chunk, 0)

    def logits(t, b_ref):
        b16 = b_ref[...].astype(BF16)

        def chunk(j, carry):
            part[t, j] = term[j] + dot(b16, rows(j), NT)
            return carry

        lax.fori_loop(0, nf, chunk, 0)
        for k in range(1, nf):
            rs_copy(t, k).start()

    def residuals(t):
        for k in range(1, nf):
            rs_copy(t, k).wait_recv()
        logit = part[t, fi]
        for k in range(1, nf):
            logit = logit + rs_buf[t, k - 1]
        mine = (labels[fi].astype(F32) - jax.nn.sigmoid(logit)).astype(BF16)
        resid[t, fi] = mine
        for k in range(1, nf):
            ag_copy(t, k, fi).start()

    def population(t):
        total = dot(resid[t, fi], rows(fi))
        for k in range(1, nf):
            source = lax.rem(fi + nf - k, nf)
            ag_copy(t, k, source).wait_recv()
            total = total + dot(resid[t, source], rows(source))
        xt_buf[t, 0] = total
        for k in range(1, nl):
            xt_copy(t, k).start()

    def population_sum(t):
        for k in range(1, nl):
            xt_copy(t, k).wait_recv()
        total = xt_buf[t, li]
        for j in range(1, nl):
            total = total + xt_buf[t, lax.rem(li + nl - j, nl)]
        return total

    def likelihood(t):
        resid_f[...] = resid[t].astype(F32)
        lik[...] = jnp.zeros_like(lik)

        def chunk(j, carry):
            m = mask[j]
            a = jnp.concatenate(
                [(resid_f[j, pl.ds(c, 1), :] * m).astype(BF16) for c in range(chains)], axis=0
            )
            lik[...] += dot(a, slope[j])
            return carry

        lax.fori_loop(0, nf, chunk, 0)

    pick_t = (
        lax.broadcasted_iota(jnp.int32, (g_own, feats), 1)
        == stride * lax.broadcasted_iota(jnp.int32, (g_own, feats), 0)
    ).astype(F32).astype(BF16)
    first = li * owned

    def prepare(j, carry):
        x = rows(j)
        st = dot(pick_t, x, NT).astype(BF16)
        slope_t[j] = jnp.concatenate([st, st], axis=0)
        slope[j] = dot(x, pick_t, NT).astype(BF16)
        mask[j] = (
            ids[j] - first == lax.broadcasted_iota(jnp.int32, (owned, width), 0)
        ).astype(F32)
        return carry

    chain = lax.broadcasted_iota(jnp.int32, (chains, 1), 0)
    step_col = jnp.zeros((chains, 1), F32)
    for c in range(chains):
        step_col = jnp.where(chain == c, step_s[c], step_col)
    half = 0.5 * step_col

    pl.semaphore_wait(barrier, nf + nl - 2)
    region_dev(0, pools, regions)
    fetch.wait()
    lax.fori_loop(0, nf, prepare, 0)
    pool_terms(pools)
    logits(0, beta)
    region_reduce(0)
    residuals(0)
    population(0)
    likelihood(0)
    for c in range(chains):
        e = step_s[c]
        m = pool_m[c] + (0.5 * e) * (lik[pl.ds(c * owned, owned), :] - dev[c])
        pool_mn[c] = m
        pools_n[c] = pools[c] + e * m
    region_gather(0)
    for c in range(chains):
        e = step_s[c]
        g = unpack(reg_all[0, c // per, c % per]) - PREC * regions[c]
        m = region_m[c] + (0.5 * e) * g
        region_mn[c] = m
        regions_n[c] = regions[c] + e * m
    region_dev(1, pools_n, regions_n)
    pool_terms(pools_n)
    mb = beta_m[...] + half * (population_sum(0) - total_feats * beta[...])
    beta_mn[...] = mb
    beta_n[...] = beta[...] + step_col * mb
    logits(1, beta_n)
    region_reduce(1)
    residuals(1)
    population(1)
    likelihood(1)
    for c in range(chains):
        pool_mn[c] = pool_mn[c] + (0.5 * step_s[c]) * (lik[pl.ds(c * owned, owned), :] - dev[c])
    region_gather(1)
    for c in range(chains):
        g = unpack(reg_all[1, c // per, c % per]) - PREC * regions_n[c]
        region_mn[c] = region_mn[c] + (0.5 * step_s[c]) * g
    beta_mn[...] = beta_mn[...] + half * (population_sum(1) - total_feats * beta_n[...])
    for t in range(2):
        for k in range(1, nf):
            rs_copy(t, k).wait_send()
            ag_copy(t, k, fi).wait_send()
        for k in range(1, nl):
            xt_copy(t, k).wait_send()
            rr_copy(t, k).wait_send()
            ra_copy(t, k, li).wait_send()


def folds(n_reg, g_own):
    return max(1, min(128 // g_own, n_reg // 8))


def emit(*refs):
    n = len(refs) // 2
    for i in range(n):
        refs[n + i][...] = refs[i][...]


def body(
    nf,
    nl,
    design,
    labels,
    pool_ids,
    pool_region_index,
    step_size,
    beta,
    pools,
    regions,
    beta_momentum,
    pool_momentum,
    region_momentum,
):
    loans, feats = design.shape
    chains, owned, g_own = pools.shape
    n_reg = regions.shape[1]
    width = loans // nf
    fold = folds(n_reg, g_own)
    packed = (n_reg // fold, fold * g_own)
    per = chains // nl
    vmem = pl.BlockSpec(memory_space=pltpu.VMEM)
    smem = pl.BlockSpec(memory_space=pltpu.SMEM)
    hbm = pl.BlockSpec(memory_space=pl.ANY)
    dma = pltpu.SemaphoreType.DMA
    args = (
        design,
        labels.reshape(nf, 1, width),
        pool_ids.reshape(nf, 1, width),
        pool_region_index.reshape(1, owned),
        step_size,
        beta,
        pools,
        regions,
        beta_momentum,
        pool_momentum,
        region_momentum,
    )
    outs = (beta, pools, regions, beta_momentum, pool_momentum, region_momentum)
    shapes = tuple(jax.ShapeDtypeStruct(x.shape, x.dtype) for x in outs)
    results = pl.pallas_call(
        functools.partial(kernel, nf, nl),
        out_shape=shapes,
        in_specs=[{0: hbm, 4: smem}.get(i, vmem) for i in range(len(args))],
        out_specs=tuple(vmem for _ in outs),
        scratch_shapes=[
            pltpu.VMEM((loans, feats), BF16),
            pltpu.VMEM((nf, owned, width), F32),
            pltpu.VMEM((nf, 2 * g_own, width), BF16),
            pltpu.VMEM((nf, width, g_own), BF16),
            pltpu.VMEM((chains * owned, 2 * g_own), BF16),
            pltpu.VMEM((chains, owned, g_own), F32),
            pltpu.VMEM((chains * owned, g_own), F32),
            pltpu.VMEM((nf, chains, width), F32),
            pltpu.VMEM((2, nf, chains, width), F32),
            pltpu.VMEM((2, nf - 1, chains, width), F32),
            pltpu.VMEM((2, nf, chains, width), BF16),
            pltpu.VMEM((nf, chains, width), F32),
            pltpu.VMEM((2, nl, chains, feats), F32),
            pltpu.VMEM((2, chains) + packed, F32),
            pltpu.VMEM((2, nl - 1, per) + packed, F32),
            pltpu.VMEM((2, per) + packed, F32),
            pltpu.VMEM((2, nl, per) + packed, F32),
            dma,
            dma((2, nf - 1)),
            dma((2, nf - 1)),
            dma((2, nf - 1)),
            dma((2, nf - 1)),
            dma((2, nl - 1)),
            dma((2, nl - 1)),
            dma((2, nl - 1)),
            dma((2, nl - 1)),
            dma((2, nl - 1)),
            dma((2, nl - 1)),
        ],
        compiler_params=pltpu.CompilerParams(
            collective_id=0, has_side_effects=True, vmem_limit_bytes=60 << 20
        ),
    )(*args)
    return pl.pallas_call(
        emit,
        out_shape=shapes,
        in_specs=[vmem] * len(shapes),
        out_specs=tuple(vmem for _ in shapes),
    )(*results)


def solution(mesh):
    in_specs = (
        P(("grp", "loan"), "feat"),
        P(("grp", "loan")),
        P(("grp", "loan")),
        P(("grp", "loan")),
        P("grp"),
        P("grp", "feat"),
        P("grp", "loan", "feat"),
        P("grp", None, "feat"),
        P("grp", "feat"),
        P("grp", "loan", "feat"),
        P("grp", None, "feat"),
    )
    out_specs = (
        P("grp", "feat"),
        P("grp", "loan", "feat"),
        P("grp", None, "feat"),
        P("grp", "feat"),
        P("grp", "loan", "feat"),
        P("grp", None, "feat"),
    )
    step = functools.partial(body, mesh.shape["feat"], mesh.shape["loan"])
    return jax.shard_map(step, mesh=mesh, in_specs=in_specs, out_specs=out_specs, check_vma=False)
```

profile of v0, /device:TPU:0, one launch (start us, length us, event | category | flops | bytes accessed | tf_op | source)
XLA Modules:
  0.0 49.3 jit_solution(15984551990605748)
XLA Ops:
  0.6 45.7 %shard_map.154 = (f32[16,1024]{1,0:T(8,128)}, f32[16,64,64]{2,1,0:T(8,128)}, f32[16,64,64]{2,1,0:T(8,128)}, f32[16,1024]{1,0:T(8,128)}, f32[16,64,64]{2,1,0:T(8,128)}, /*index=5*/f32[16,64,64]{2,1,0:T(8,128)}) custom-call(bf16[2048,1024]{1,0:T(8,128)(2,1)} %design_hbm.1, s32[4,1,512]{2,1,0:T(1,128)} %bitcast.3, s32[4,1,512]{2,1,0:T(1,128)} %bitcast.4, ...), custom_call_target="tpu_custom_call" | custom-call | tf_op jit(solution)/shard_map/pallas_call | solution.py:394
  46.3 2.9 %shard_map.155 = (f32[16,1024]{1,0:T(8,128)}, f32[16,64,64]{2,1,0:T(8,128)}, f32[16,64,64]{2,1,0:T(8,128)}, f32[16,1024]{1,0:T(8,128)}, f32[16,64,64]{2,1,0:T(8,128)}, /*index=5*/f32[16,64,64]{2,1,0:T(8,128)}) custom-call(f32[16,1024]{1,0:T(8,128)} %get-tuple-element.12.refs_0_, f32[16,64,64]{2,1,0:T(8,128)} %get-tuple-element.13.refs_1_, ...), custom_call_target="tpu_custom_call" | custom-call | tf_op jit(solution)/shard_map/pallas_call | solution.py:433
where the time goes:
time: 49.4 us; the launch traced here: 49.3 us
  Pallas kernels  48.6 us (98%)
  between operations  0.64 us (1%)
    pallas_call x1, Pallas kernels, body(): pl.pallas_call(functools.partial(kernel, nf, nl), out_shape=shapes, in_sp...  45.7 us
    pallas_call x1, Pallas kernels, body(): pl.pallas_call(emit, out_shape=shapes, in_specs=[vmem] * len(shapes), out...  2.95 us

commit v1 on v0

v1 whole, which is shorter than its diff:
```python
import functools

import jax
import jax.numpy as jnp
from jax import lax
from jax.experimental import pallas as pl
from jax.experimental.pallas import tpu as pltpu
from jax.sharding import PartitionSpec as P

PREC = 256.0
MESH = pl.DeviceIdType.MESH
NT = (((1,), (1,)), ((), ()))
NN = (((1,), (0,)), ((), ()))
F32 = jnp.float32
BF16 = jnp.bfloat16


def dot(a, b, dims=NN):
    return lax.dot_general(a, b, dims, preferred_element_type=F32)


def halves(x):
    hi = x.astype(BF16)
    return hi, (x - hi.astype(F32)).astype(BF16)


def blocks_of(owned, g_own):
    return max(1, min(256 // g_own, owned // 16))


def kernel(
    nf,
    nl,
    design_hbm,
    labels_hbm,
    ids_hbm,
    pri_hbm,
    step_hbm,
    beta_hbm,
    pools_hbm,
    regions_hbm,
    beta_m_hbm,
    pool_m_hbm,
    region_m_hbm,
    beta_n,
    pools_n,
    regions_n,
    beta_mn,
    pool_mn,
    region_mn,
    design,
    labels,
    ids,
    pri,
    step_s,
    beta,
    pools,
    regions,
    beta_m,
    pool_m,
    region_m,
    lhs,
    mask,
    fold,
    u4,
    lik,
    term,
    dev,
    part,
    rs_buf,
    resid,
    resid_f,
    xt_buf,
    reg_part,
    reg_buf,
    reg_all,
    load,
    load_d,
    s_rs,
    r_rs,
    s_ag,
    r_ag,
    s_xt,
    r_xt,
    s_rr,
    r_rr,
    s_ra,
    r_ra,
    s_pr,
    r_pr,
):
    fi = lax.axis_index("feat")
    li = lax.axis_index("loan")
    chains, owned, g_own = pools.shape
    feats = beta.shape[1]
    n_reg = regions.shape[1]
    width = labels.shape[2]
    stride = feats // g_own
    total_feats = float(feats * nf)
    nb = blocks_of(owned, g_own)
    prow = owned // nb
    lanes = chains * g_own
    side = max(1, 128 // g_own)
    span = side * g_own
    nx = nf // 2
    order = [k for k in range(2, nf)] + [1, 0]
    arrive = [0, 1] + [k for k in range(2, nf)]

    def peer_of(k):
        return lax.rem(fi // 2 + k // 2, nx) * 2 + lax.rem(fi + k, 2)

    def source_of(k):
        return lax.rem(fi // 2 + nx - k // 2, nx) * 2 + lax.rem(fi + k, 2)

    def fetch_rows(k):
        j = peer_of(k)
        return pltpu.make_async_copy(
            design_hbm.at[pl.ds(pl.multiple_of(j * width, width), width), :],
            design.at[j],
            load_d.at[k],
        )

    def fetch(i):
        src, dst = (
            (beta_hbm, beta),
            (ids_hbm, ids),
            (pools_hbm, pools),
            (labels_hbm, labels),
            (pri_hbm, pri.at[li]),
            (step_hbm, step_s),
            (regions_hbm, regions),
            (pool_m_hbm, pool_m),
            (region_m_hbm, region_m),
            (beta_m_hbm, beta_m),
        )[i]
        return pltpu.make_async_copy(src, dst, load.at[i])

    for i in range(2):
        fetch(i).start()
    fetch_rows(order[0]).start()
    fetch(2).start()
    for k in order[1:]:
        fetch_rows(k).start()
    for i in range(3, 10):
        fetch(i).start()

    barrier = pltpu.get_barrier_semaphore()
    for k in range(1, nf):
        pl.semaphore_signal(
            barrier, inc=1, device_id={"feat": peer_of(k)}, device_id_type=MESH
        )
    for k in range(1, nl):
        pl.semaphore_signal(
            barrier, inc=1, device_id={"loan": lax.rem(li + k, nl)}, device_id_type=MESH
        )

    def remote(src, dst, ss, rs, axis, peer):
        return pltpu.make_async_remote_copy(
            src_ref=src,
            dst_ref=dst,
            send_sem=ss,
            recv_sem=rs,
            device_id={axis: peer},
            device_id_type=MESH,
        )

    def rs_copy(t, k):
        peer = peer_of(k)
        return remote(
            part.at[t, peer], rs_buf.at[t, k - 1], s_rs.at[t, k - 1], r_rs.at[t, k - 1], "feat", peer
        )

    def ag_copy(t, k, slot):
        return remote(
            resid.at[t, slot],
            resid.at[t, slot],
            s_ag.at[t, k - 1],
            r_ag.at[t, k - 1],
            "feat",
            peer_of(k),
        )

    def loan_peer(k):
        return lax.rem(li + k, nl)

    def loan_source(k):
        return lax.rem(li + nl - k, nl)

    def xt_copy(t, k):
        return remote(
            xt_buf.at[t, 0],
            xt_buf.at[t, k],
            s_xt.at[t, k - 1],
            r_xt.at[t, k - 1],
            "loan",
            loan_peer(k),
        )

    def rr_copy(t, k):
        peer = loan_peer(k)
        return remote(
            reg_part.at[t, peer], reg_buf.at[t, k - 1], s_rr.at[t, k - 1], r_rr.at[t, k - 1], "loan", peer
        )

    def ra_copy(t, k, owner):
        return remote(
            reg_all.at[t, owner],
            reg_all.at[t, owner],
            s_ra.at[t, k - 1],
            r_ra.at[t, k - 1],
            "loan",
            loan_peer(k),
        )

    def pr_copy(k, owner):
        return remote(
            pri.at[owner], pri.at[owner], s_pr.at[k - 1], r_pr.at[k - 1], "loan", loan_peer(k)
        )

    def onehot_t(row):
        return (row == lax.broadcasted_iota(jnp.int32, (n_reg, owned), 0)).astype(F32)

    def wide(ref, i):
        return jnp.concatenate([ref[i * side + c] for c in range(side)], axis=1)

    def cols(i):
        return pl.ds(i * span, span)

    n_cols = lanes // span

    def prologue():
        fetch(0).wait()
        lhs[pl.ds(0, chains), :] = beta[...].astype(BF16)
        lhs[pl.ds(chains, g_own), :] = (
            (
                lax.broadcasted_iota(jnp.int32, (g_own, feats), 1)
                == stride * lax.broadcasted_iota(jnp.int32, (g_own, feats), 0)
            )
            .astype(F32)
            .astype(BF16)
        )
        fetch(1).wait()

    def put_u4(c, blocks):
        hi, lo = halves(jnp.concatenate(blocks, axis=1))
        u4[pl.ds(c * prow, prow), :] = hi
        u4[pl.ds((chains + c) * prow, prow), :] = lo

    def slopes_first():
        fetch(2).wait()
        for c in range(chains):
            put_u4(c, [pools[c, pl.ds(k * prow, prow), :] for k in range(nb)])

    def slopes_next():
        for c in range(chains):
            put_u4(
                c,
                [
                    pools_n[pl.ds(k * prow, prow), pl.ds(c * g_own, g_own)]
                    for k in range(nb)
                ],
            )

    def pool_term(j):
        z = dot(u4[...], fold[j])
        m = mask[j]
        low = chains * prow
        for c in range(chains):
            a = z[c * prow : (c + 1) * prow] + z[low + c * prow : low + (c + 1) * prow]
            term[j, pl.ds(c, 1), :] = jnp.sum(a * m, axis=0, keepdims=True)

    first = li * owned

    def logits_first(k):
        j = peer_of(k)
        fetch_rows(k).wait()
        both = dot(lhs[...], design[j], NT)
        local = ids[j] - first
        block = local // prow
        mask[j] = (
            local - block * prow == lax.broadcasted_iota(jnp.int32, (prow, width), 0)
        ).astype(F32)
        slope = both[chains:]
        for b in range(nb):
            fold[j, pl.ds(b * g_own, g_own), :] = jnp.where(block == b, slope, 0.0).astype(BF16)
        pool_term(j)
        part[0, j] = term[j] + both[:chains]
        if k:
            rs_copy(0, k).start()

    def terms_next():
        def chunk(j, carry):
            pool_term(j)
            return carry

        lax.fori_loop(0, nf, chunk, 0)

    def logits_next():
        b16 = beta_n[...].astype(BF16)
        for k in order:
            j = peer_of(k)
            part[1, j] = term[j] + dot(b16, design[j], NT)
            if k:
                rs_copy(1, k).start()

    def residuals(t):
        logit = part[t, fi]
        for k in range(1, nf):
            rs_copy(t, k).wait_recv()
            logit = logit + rs_buf[t, k - 1]
        mine = (labels[fi].astype(F32) - jax.nn.sigmoid(logit)).astype(BF16)
        resid[t, fi] = mine
        for k in order[:-1]:
            ag_copy(t, k, fi).start()

    def population(t, k):
        s = source_of(k)
        if k:
            ag_copy(t, k, s).wait_recv()
        x = dot(resid[t, s], design[s])
        if k == arrive[0]:
            xt_buf[t, 0] = x
        else:
            xt_buf[t, 0] += x

    def population_send(t):
        for k in range(1, nl):
            xt_copy(t, k).start()

    def population_sum(t):
        for k in range(1, nl):
            xt_copy(t, k).wait_recv()
        total = xt_buf[t, li]
        for j in range(1, nl):
            total = total + xt_buf[t, lax.rem(li + nl - j, nl)]
        return total

    def likelihood(t, k):
        s = source_of(k)
        resid_f[...] = resid[t, s].astype(F32)
        m = mask[s]
        a = jnp.concatenate(
            [(resid_f[pl.ds(c, 1), :] * m).astype(BF16) for c in range(chains)], axis=0
        )
        x = dot(a, fold[s], NT)
        if k == arrive[0]:
            lik[...] = x
        else:
            lik[...] += x

    def lik_cols(i):
        return jnp.concatenate(
            [
                jnp.concatenate(
                    [
                        lik[
                            pl.ds((i * side + c) * prow, prow), pl.ds(k * g_own, g_own)
                        ]
                        for c in range(side)
                    ],
                    axis=1,
                )
                for k in range(nb)
            ],
            axis=0,
        )

    def step_cols(i):
        lane = lax.broadcasted_iota(jnp.int32, (1, span), 1) // g_own
        e = jnp.zeros((1, span), F32)
        for c in range(side):
            e = jnp.where(lane == c, step_s[i * side + c], e)
        return e

    def region_sum(t, get):
        oht = onehot_t(pri[li])
        oht2 = jnp.concatenate([oht, oht], axis=1).astype(BF16)
        rows = n_reg // nl
        for i in range(n_cols):
            hi, lo = halves(get(i))
            s = dot(oht2, jnp.concatenate([hi, lo], axis=0))
            for o in range(nl):
                reg_part[t, o, :, cols(i)] = s[o * rows : (o + 1) * rows]

    def region_send(t):
        for k in range(1, nl):
            rr_copy(t, k).start()

    def deviation(get_u, get_v):
        oht = onehot_t(pri[li])
        eye = (
            lax.broadcasted_iota(jnp.int32, (owned, owned), 0)
            == lax.broadcasted_iota(jnp.int32, (owned, owned), 1)
        ).astype(F32)
        oh = dot(eye.astype(BF16), oht.astype(BF16), NT)
        oh2 = jnp.concatenate([oh, oh], axis=1).astype(BF16)
        for i in range(n_cols):
            hi, lo = halves(get_v(i))
            dev[:, cols(i)] = PREC * (get_u(i) - dot(oh2, jnp.concatenate([hi, lo], axis=0)))

    def region_first():
        fetch(4).wait()
        region_sum(0, lambda i: wide(pools, i))
        for k in range(1, nl):
            pr_copy(k, li).start()
        region_send(0)

    def deviation_first():
        fetch(6).wait()
        deviation(lambda i: wide(pools, i), lambda i: wide(regions, i))

    def region_reduce(t):
        total = reg_part[t, li]
        for k in range(1, nl):
            rr_copy(t, k).wait_recv()
            total = total + reg_buf[t, k - 1]
        reg_all[t, li] = total
        for k in range(1, nl):
            ra_copy(t, k, li).start()

    def region_gather(t):
        for k in range(1, nl):
            ra_copy(t, k, loan_source(k)).wait_recv()

    def counts():
        n = jnp.zeros((n_reg, 1), F32)
        for i in range(nl):
            n = n + jnp.sum(onehot_t(pri[i]), axis=1, keepdims=True)
        return n + 1.0

    def region_force(t, i, get_v, n):
        s = jnp.concatenate([reg_all[t, o, :, cols(i)] for o in range(nl)], axis=0)
        return PREC * (s - n * get_v(i))

    def wait_rest():
        fetch(3).wait()
        fetch(5).wait()

    def pool_update():
        fetch(7).wait()
        for i in range(n_cols):
            e = step_cols(i)
            m = wide(pool_m, i) + (0.5 * e) * (lik_cols(i) - dev[:, cols(i)])
            pool_mn[:, cols(i)] = m
            pools_n[:, cols(i)] = wide(pools, i) + e * m

    def region_next():
        fetch(8).wait()
        region_gather(0)
        for k in range(1, nl):
            pr_copy(k, loan_source(k)).wait_recv()
        n = counts()
        for i in range(n_cols):
            e = step_cols(i)
            g = region_force(0, i, lambda i: wide(regions, i), n)
            m = wide(region_m, i) + (0.5 * e) * g
            region_mn[:, cols(i)] = m
            regions_n[:, cols(i)] = wide(regions, i) + e * m
        deviation(lambda i: pools_n[:, cols(i)], lambda i: regions_n[:, cols(i)])

    def region_last():
        region_gather(1)
        n = counts()
        for i in range(n_cols):
            g = region_force(1, i, lambda i: regions_n[:, cols(i)], n)
            region_mn[:, cols(i)] += (0.5 * step_cols(i)) * g

    def pool_last():
        for i in range(n_cols):
            pool_mn[:, cols(i)] += (0.5 * step_cols(i)) * (lik_cols(i) - dev[:, cols(i)])

    def step_rows():
        chain = lax.broadcasted_iota(jnp.int32, (chains, 1), 0)
        e = jnp.zeros((chains, 1), F32)
        for c in range(chains):
            e = jnp.where(chain == c, step_s[c], e)
        return e

    def beta_next():
        fetch(9).wait()
        e = step_rows()
        m = beta_m[...] + (0.5 * e) * (population_sum(0) - total_feats * beta[...])
        beta_mn[...] = m
        beta_n[...] = beta[...] + e * m

    def beta_last():
        beta_mn[...] += (0.5 * step_rows()) * (population_sum(1) - total_feats * beta_n[...])

    def barrier_wait():
        pl.semaphore_wait(barrier, nf + nl - 2)

    def sum_next():
        region_sum(1, lambda i: pools_n[:, cols(i)])
        region_send(1)

    def sent():
        for t in range(2):
            for k in range(1, nf):
                rs_copy(t, k).wait_send()
                ag_copy(t, k, fi).wait_send()
            for k in range(1, nl):
                xt_copy(t, k).wait_send()
                rr_copy(t, k).wait_send()
                ra_copy(t, k, li).wait_send()
        for k in range(1, nl):
            pr_copy(k, li).wait_send()

    prologue()
    slopes_first()
    barrier_wait()
    for k in order:
        logits_first(k)
    region_first()
    deviation_first()
    wait_rest()
    residuals(0)
    for k in arrive[:2]:
        population(0, k)
        likelihood(0, k)
    region_reduce(0)
    for k in arrive[2:]:
        population(0, k)
    population_send(0)
    for k in arrive[2:]:
        likelihood(0, k)
    pool_update()
    slopes_next()
    terms_next()
    sum_next()
    beta_next()
    logits_next()
    region_next()
    residuals(1)
    for k in arrive[:2]:
        population(1, k)
        likelihood(1, k)
    region_reduce(1)
    for k in arrive[2:]:
        population(1, k)
    population_send(1)
    for k in arrive[2:]:
        likelihood(1, k)
    pool_last()
    region_last()
    beta_last()
    sent()


def emit(
    beta_n,
    pools_n,
    regions_n,
    beta_mn,
    pool_mn,
    region_mn,
    beta_o,
    pools_o,
    regions_o,
    beta_mo,
    pool_mo,
    region_mo,
    pools_v,
    regions_v,
    pool_mv,
    region_mv,
    sem,
):
    pending = [
        pltpu.make_async_copy(beta_n, beta_o, sem.at[0]),
        pltpu.make_async_copy(beta_mn, beta_mo, sem.at[1]),
    ]
    for copy in pending:
        copy.start()
    wide = (
        (pools_n, pools_v, pools_o),
        (regions_n, regions_v, regions_o),
        (pool_mn, pool_mv, pool_mo),
        (region_mn, region_mv, region_mo),
    )
    for n, (src, tmp, dst) in enumerate(wide):
        chains, _, g_own = tmp.shape
        for c in range(chains):
            tmp[c] = src[:, pl.ds(c * g_own, g_own)]
        copy = pltpu.make_async_copy(tmp, dst, sem.at[2 + n])
        copy.start()
        pending.append(copy)
    for copy in pending:
        copy.wait()


def body(
    nf,
    nl,
    design,
    labels,
    pool_ids,
    pool_region_index,
    step_size,
    beta,
    pools,
    regions,
    beta_momentum,
    pool_momentum,
    region_momentum,
):
    loans, feats = design.shape
    chains, owned, g_own = pools.shape
    n_reg = regions.shape[1]
    width = loans // nf
    lanes = chains * g_own
    nb = blocks_of(owned, g_own)
    prow = owned // nb
    rows = n_reg // nl
    vmem = pl.BlockSpec(memory_space=pltpu.VMEM)
    hbm = pl.BlockSpec(memory_space=pltpu.HBM)
    dma = pltpu.SemaphoreType.DMA
    args = (
        design,
        labels.reshape(nf, 1, width),
        pool_ids.reshape(nf, 1, width),
        pool_region_index.reshape(1, owned),
        step_size,
        beta,
        pools,
        regions,
        beta_momentum,
        pool_momentum,
        region_momentum,
    )
    outs = (beta, pools, regions, beta_momentum, pool_momentum, region_momentum)
    packed = tuple(
        OUT(x.shape if x.ndim == 2 else (x.shape[1], lanes), F32) for x in outs
    )
    results = pl.pallas_call(
        functools.partial(kernel, nf, nl),
        out_shape=packed,
        in_specs=[hbm] * len(args),
        out_specs=tuple(vmem for _ in outs),
        scratch_shapes=[
            pltpu.VMEM((nf, width, feats), BF16),
            pltpu.VMEM((nf, 1, width), jnp.int32),
            pltpu.VMEM((nf, 1, width), jnp.int32),
            pltpu.VMEM((nl, 1, owned), jnp.int32),
            pltpu.SMEM(step_size.shape, F32),
            pltpu.VMEM(beta.shape, F32),
            pltpu.VMEM(pools.shape, F32),
            pltpu.VMEM(regions.shape, F32),
            pltpu.VMEM(beta.shape, F32),
            pltpu.VMEM(pools.shape, F32),
            pltpu.VMEM(regions.shape, F32),
            pltpu.VMEM((chains + g_own, feats), BF16),
            pltpu.VMEM((nf, prow, width), F32),
            pltpu.VMEM((nf, nb * g_own, width), BF16),
            pltpu.VMEM((2 * chains * prow, nb * g_own), BF16),
            pltpu.VMEM((chains * prow, nb * g_own), F32),
            pltpu.VMEM((nf, chains, width), F32),
            pltpu.VMEM((owned, lanes), F32),
            pltpu.VMEM((2, nf, chains, width), F32),
            pltpu.VMEM((2, nf - 1, chains, width), F32),
            pltpu.VMEM((2, nf, chains, width), BF16),
            pltpu.VMEM((chains, width), F32),
            pltpu.VMEM((2, nl, chains, feats), F32),
            pltpu.VMEM((2, nl, rows, lanes), F32),
            pltpu.VMEM((2, nl - 1, rows, lanes), F32),
            pltpu.VMEM((2, nl, rows, lanes), F32),
            dma((10,)),
            dma((nf,)),
            dma((2, nf - 1)),
            dma((2, nf - 1)),
            dma((2, nf - 1)),
            dma((2, nf - 1)),
            dma((2, nl - 1)),
            dma((2, nl - 1)),
            dma((2, nl - 1)),
            dma((2, nl - 1)),
            dma((2, nl - 1)),
            dma((2, nl - 1)),
            dma((nl - 1,)),
            dma((nl - 1,)),
        ],
        compiler_params=pltpu.CompilerParams(
            collective_id=0, has_side_effects=True, vmem_limit_bytes=VLIM << 20
        ),
    )(*[pltpu.with_memory_space_constraint(x, pltpu.HBM) for x in args])
    return pl.pallas_call(
        emit,
        out_shape=tuple(jax.ShapeDtypeStruct(x.shape, x.dtype) for x in outs),
        in_specs=[vmem] * len(outs),
        out_specs=tuple(hbm for _ in outs),
        scratch_shapes=[
            pltpu.VMEM(pools.shape, F32),
            pltpu.VMEM(regions.shape, F32),
            pltpu.VMEM(pools.shape, F32),
            pltpu.VMEM(regions.shape, F32),
            dma((6,)),
        ],
        compiler_params=pltpu.CompilerParams(vmem_limit_bytes=16 << 20),
    )(*results)


VLIM = 24
OUT = pltpu.VMEM


def solution(mesh):
    in_specs = (
        P(("grp", "loan"), "feat"),
        P(("grp", "loan")),
        P(("grp", "loan")),
        P(("grp", "loan")),
        P("grp"),
        P("grp", "feat"),
        P("grp", "loan", "feat"),
        P("grp", None, "feat"),
        P("grp", "feat"),
        P("grp", "loan", "feat"),
        P("grp", None, "feat"),
    )
    out_specs = (
        P("grp", "feat"),
        P("grp", "loan", "feat"),
        P("grp", None, "feat"),
        P("grp", "feat"),
        P("grp", "loan", "feat"),
        P("grp", None, "feat"),
    )
    step = functools.partial(body, mesh.shape["feat"], mesh.shape["loan"])
    return jax.shard_map(step, mesh=mesh, in_specs=in_specs, out_specs=out_specs, check_vma=False)
```

time: 49.4 us -> 50.4 us (1.020)
  Pallas kernels: 48.6 us -> 49.6 us
    pallas_call x2, Pallas kernels: 48.6 us -> 49.6 us  [the longest x1 47.9 us: body(): pl.pallas_call(functools.partial(kernel, nf, nl), out_shape=packed, in_sp...]
where the time goes in v1:
time: 50.4 us; the launch traced here: 50.2 us
  Pallas kernels  49.6 us (98%)
  between operations  0.64 us (1%)
    pallas_call x1, Pallas kernels, body(): pl.pallas_call(functools.partial(kernel, nf, nl), out_shape=packed, in_sp...  47.9 us
    pallas_call x1, Pallas kernels, body(): pl.pallas_call(emit, out_shape=tuple((jax.ShapeDtypeStruct(x.shape, x.dty...  1.64 us

profile of v1, /device:TPU:0, one launch (start us, length us, event | category | flops | bytes accessed | tf_op | source)
XLA Modules:
  0.0 50.2 jit_solution(10780869478166983844)
XLA Ops:
  0.6 47.9 %shard_map.154 = (f32[16,1024]{1,0:T(8,128)S(1)}, f32[64,1024]{1,0:T(8,128)S(1)}, f32[64,1024]{1,0:T(8,128)S(1)}, f32[16,1024]{1,0:T(8,128)S(1)}, f32[64,1024]{1,0:T(8,128)S(1)}, /*index=5*/f32[64,1024]{1,0:T(8,128)S(1)}) custom-call(bf16[2048,1024]{1,0:T(8,128)(2,1)} %design_hbm.1, s32[4,1,512]{2,1,0:T(1,128)} %bitcast.3, s32[4,1,512]{2,1,0:T(1,128)} %bitcast.4, ...), custom_call_target="tpu_custom_call" | custom-call | tf_op jit(solution)/shard_map/pallas_call | solution.py:634
  48.6 1.6 %shard_map.155 = (f32[16,1024]{1,0:T(8,128)}, f32[16,64,64]{2,1,0:T(8,128)}, f32[16,64,64]{2,1,0:T(8,128)}, f32[16,1024]{1,0:T(8,128)}, f32[16,64,64]{2,1,0:T(8,128)}, /*index=5*/f32[16,64,64]{2,1,0:T(8,128)}) custom-call(f32[16,1024]{1,0:T(8,128)S(1)} %get-tuple-element.12.beta_n, f32[64,1024]{1,0:T(8,128)S(1)} %get-tuple-element.13.pools_n, ...), custom_call_target="tpu_custom_call" | custom-call | tf_op jit(solution)/shard_map/pallas_call | solution.py:685

commit v2 on v1

--- a/solution.py
+++ b/solution.py
@@ -13,6 +13,8 @@
 NN = (((1,), (0,)), ((), ()))
 F32 = jnp.float32
 BF16 = jnp.bfloat16
+I16 = jnp.int16
+TOP = 32767.0
 
 
 def dot(a, b, dims=NN):
@@ -22,6 +24,17 @@
 def halves(x):
     hi = x.astype(BF16)
     return hi, (x - hi.astype(F32)).astype(BF16)
+
+
+def code(x):
+    top = jnp.max(jnp.abs(x), axis=0, keepdims=True)
+    top = jnp.maximum(top, 1e-30)
+    q = jnp.round(x * (TOP / top)).astype(jnp.int32).astype(I16)
+    return q, top * (1.0 / TOP)
+
+
+def decode(q, scale):
+    return q.astype(jnp.int32).astype(F32) * scale
 
 
 def blocks_of(owned, g_own):
@@ -70,10 +83,17 @@
     rs_buf,
     resid,
     resid_f,
-    xt_buf,
-    reg_part,
-    reg_buf,
-    reg_all,
+    xt_f,
+    xt_q,
+    xt_s,
+    part_q,
+    part_s,
+    buf_q,
+    buf_s,
+    all_q,
+    all_s,
+    flipped,
+    eye,
     load,
     load_d,
     s_rs,
@@ -186,31 +206,45 @@
     def loan_source(k):
         return lax.rem(li + nl - k, nl)
 
-    def xt_copy(t, k):
-        return remote(
-            xt_buf.at[t, 0],
-            xt_buf.at[t, k],
-            s_xt.at[t, k - 1],
-            r_xt.at[t, k - 1],
-            "loan",
-            loan_peer(k),
-        )
-
-    def rr_copy(t, k):
+    def xt_copies(t, k):
+        return [
+            remote(
+                ref.at[t, 0],
+                ref.at[t, k],
+                s_xt.at[i, t, k - 1],
+                r_xt.at[i, t, k - 1],
+                "loan",
+                loan_peer(k),
+            )
+            for i, ref in enumerate((xt_s, xt_q))
+        ]
+
+    def rr_copies(t, k):
         peer = loan_peer(k)
-        return remote(
-            reg_part.at[t, peer], reg_buf.at[t, k - 1], s_rr.at[t, k - 1], r_rr.at[t, k - 1], "loan", peer
-        )
-
-    def ra_copy(t, k, owner):
-        return remote(
-            reg_all.at[t, owner],
-            reg_all.at[t, owner],
-            s_ra.at[t, k - 1],
-            r_ra.at[t, k - 1],
-            "loan",
-            loan_peer(k),
-        )
+        return [
+            remote(
+                src.at[t, peer],
+                dst.at[t, k - 1],
+                s_rr.at[i, t, k - 1],
+                r_rr.at[i, t, k - 1],
+                "loan",
+                peer,
+            )
+            for i, (src, dst) in enumerate(((part_s, buf_s), (part_q, buf_q)))
+        ]
+
+    def ra_copies(t, k, owner):
+        return [
+            remote(
+                ref.at[t, owner],
+                ref.at[t, owner],
+                s_ra.at[i, t, k - 1],
+                r_ra.at[i, t, k - 1],
+                "loan",
+                loan_peer(k),
+            )
+            for i, ref in enumerate((all_s, all_q))
+        ]
 
     def pr_copy(k, owner):
         return remote(
@@ -235,6 +269,15 @@
             (
                 lax.broadcasted_iota(jnp.int32, (g_own, feats), 1)
                 == stride * lax.broadcasted_iota(jnp.int32, (g_own, feats), 0)
+            )
+            .astype(F32)
+            .astype(BF16)
+        )
+        size = eye.shape[0]
+        eye[...] = (
+            (
+                lax.broadcasted_iota(jnp.int32, (size, size), 0)
+                == lax.broadcasted_iota(jnp.int32, (size, size), 1)
             )
             .astype(F32)
             .astype(BF16)
@@ -289,17 +332,21 @@
             rs_copy(0, k).start()
 
     def terms_next():
-        def chunk(j, carry):
+        for j in range(nf):
             pool_term(j)
-            return carry
-
-        lax.fori_loop(0, nf, chunk, 0)
+
+    def flip(k):
+        j = peer_of(k)
+        size = eye.shape[0]
+        for i in range(feats // size):
+            x = dot(eye[...], design[j, :, pl.ds(i * size, size)], NT)
+            flipped[j, pl.ds(i * size, size), :] = x.astype(BF16)
 
     def logits_next():
         b16 = beta_n[...].astype(BF16)
         for k in order:
             j = peer_of(k)
-            part[1, j] = term[j] + dot(b16, design[j], NT)
+            part[1, j] = term[j] + dot(b16, flipped[j])
             if k:
                 rs_copy(1, k).start()
 
@@ -319,20 +366,25 @@
             ag_copy(t, k, s).wait_recv()
         x = dot(resid[t, s], design[s])
         if k == arrive[0]:
-            xt_buf[t, 0] = x
+            xt_f[...] = x
+        elif k != arrive[-1]:
+            xt_f[...] += x
         else:
-            xt_buf[t, 0] += x
+            xt_q[t, 0], xt_s[t, 0] = code(xt_f[...] + x)
 
     def population_send(t):
         for k in range(1, nl):
-            xt_copy(t, k).start()
+            for copy in xt_copies(t, k):
+                copy.start()
 
     def population_sum(t):
         for k in range(1, nl):
-            xt_copy(t, k).wait_recv()
-        total = xt_buf[t, li]
+            for copy in xt_copies(t, k):
+                copy.wait_recv()
+        total = decode(xt_q[t, li], xt_s[t, li])
         for j in range(1, nl):
-            total = total + xt_buf[t, lax.rem(li + nl - j, nl)]
+            slot = lax.rem(li + nl - j, nl)
+            total = total + decode(xt_q[t, slot], xt_s[t, slot])
         return total
 
     def likelihood(t, k):
@@ -380,11 +432,14 @@
             hi, lo = halves(get(i))
             s = dot(oht2, jnp.concatenate([hi, lo], axis=0))
             for o in range(nl):
-                reg_part[t, o, :, cols(i)] = s[o * rows : (o + 1) * rows]
+                q, scale = code(s[o * rows : (o + 1) * rows])
+                part_q[t, o, :, cols(i)] = q
+                part_s[t, o, :, cols(i)] = scale
 
     def region_send(t):
         for k in range(1, nl):
-            rr_copy(t, k).start()
+            for copy in rr_copies(t, k):
+                copy.start()
 
     def deviation(get_u, get_v):
         oht = onehot_t(pri[li])
@@ -410,17 +465,20 @@
         deviation(lambda i: wide(pools, i), lambda i: wide(regions, i))
 
     def region_reduce(t):
-        total = reg_part[t, li]
-        for k in range(1, nl):
-            rr_copy(t, k).wait_recv()
-            total = total + reg_buf[t, k - 1]
-        reg_all[t, li] = total
-        for k in range(1, nl):
-            ra_copy(t, k, li).start()
+        total = decode(part_q[t, li], part_s[t, li])
+        for k in range(1, nl):
+            for copy in rr_copies(t, k):
+                copy.wait_recv()
+            total = total + decode(buf_q[t, k - 1], buf_s[t, k - 1])
+        all_q[t, li], all_s[t, li] = code(total)
+        for k in range(1, nl):
+            for copy in ra_copies(t, k, li):
+                copy.start()
 
     def region_gather(t):
         for k in range(1, nl):
-            ra_copy(t, k, loan_source(k)).wait_recv()
+            for copy in ra_copies(t, k, loan_source(k)):
+                copy.wait_recv()
 
     def counts():
         n = jnp.zeros((n_reg, 1), F32)
@@ -429,7 +487,9 @@
         return n + 1.0
 
     def region_force(t, i, get_v, n):
-        s = jnp.concatenate([reg_all[t, o, :, cols(i)] for o in range(nl)], axis=0)
+        s = jnp.concatenate(
+            [decode(all_q[t, o, :, cols(i)], all_s[t, o, :, cols(i)]) for o in range(nl)], axis=0
+        )
         return PREC * (s - n * get_v(i))
 
     def wait_rest():
@@ -499,9 +559,8 @@
                 rs_copy(t, k).wait_send()
                 ag_copy(t, k, fi).wait_send()
             for k in range(1, nl):
-                xt_copy(t, k).wait_send()
-                rr_copy(t, k).wait_send()
-                ra_copy(t, k, li).wait_send()
+                for copy in xt_copies(t, k) + rr_copies(t, k) + ra_copies(t, k, li):
+                    copy.wait_send()
         for k in range(1, nl):
             pr_copy(k, li).wait_send()
 
@@ -517,7 +576,7 @@
     for k in arrive[:2]:
         population(0, k)
         likelihood(0, k)
-    region_reduce(0)
+    flip(arrive[0])
     for k in arrive[2:]:
         population(0, k)
     population_send(0)
@@ -527,13 +586,16 @@
     slopes_next()
     terms_next()
     sum_next()
+    for k in arrive[1:]:
+        flip(k)
+    region_reduce(0)
     beta_next()
     logits_next()
-    region_next()
     residuals(1)
     for k in arrive[:2]:
         population(1, k)
         likelihood(1, k)
+    region_next()
     region_reduce(1)
     for k in arrive[2:]:
         population(1, k)
@@ -659,22 +721,29 @@
             pltpu.VMEM((2, nf - 1, chains, width), F32),
             pltpu.VMEM((2, nf, chains, width), BF16),
             pltpu.VMEM((chains, width), F32),
-            pltpu.VMEM((2, nl, chains, feats), F32),
-            pltpu.VMEM((2, nl, rows, lanes), F32),
-            pltpu.VMEM((2, nl - 1, rows, lanes), F32),
-            pltpu.VMEM((2, nl, rows, lanes), F32),
+            pltpu.VMEM((chains, feats), F32),
+            pltpu.VMEM((2, nl, chains, feats), I16),
+            pltpu.VMEM((2, nl, 1, feats), F32),
+            pltpu.VMEM((2, nl, rows, lanes), I16),
+            pltpu.VMEM((2, nl, 1, lanes), F32),
+            pltpu.VMEM((2, nl - 1, rows, lanes), I16),
+            pltpu.VMEM((2, nl - 1, 1, lanes), F32),
+            pltpu.VMEM((2, nl, rows, lanes), I16),
+            pltpu.VMEM((2, nl, 1, lanes), F32),
+            pltpu.VMEM((nf, feats, width), BF16),
+            pltpu.VMEM((min(256, feats),) * 2, BF16),
             dma((10,)),
             dma((nf,)),
             dma((2, nf - 1)),
             dma((2, nf - 1)),
             dma((2, nf - 1)),
             dma((2, nf - 1)),
-            dma((2, nl - 1)),
-            dma((2, nl - 1)),
-            dma((2, nl - 1)),
-            dma((2, nl - 1)),
-            dma((2, nl - 1)),
-            dma((2, nl - 1)),
+            dma((2, 2, nl - 1)),
+            dma((2, 2, nl - 1)),
+            dma((2, 2, nl - 1)),
+            dma((2, 2, nl - 1)),
+            dma((2, 2, nl - 1)),
+            dma((2, 2, nl - 1)),
             dma((nl - 1,)),
             dma((nl - 1,)),
         ],

time: 50.4 us -> 35.2 us (0.70)
  Pallas kernels: 49.6 us -> 34.4 us
    pallas_call x1, Pallas kernels: 47.9 us -> 32.8 us  [body(): pl.pallas_call(functools.partial(kernel, nf, nl), out_shape=packed, in_sp...]
where the time goes in v2:
time: 35.2 us; the launch traced here: 35 us
  Pallas kernels  34.4 us (98%)
  between operations  0.64 us (2%)
    pallas_call x1, Pallas kernels, body(): pl.pallas_call(functools.partial(kernel, nf, nl), out_shape=packed, in_sp...  32.8 us
    pallas_call x1, Pallas kernels, body(): pl.pallas_call(emit, out_shape=tuple((jax.ShapeDtypeStruct(x.shape, x.dty...  1.64 us

profile of v2, /device:TPU:0, one launch (start us, length us, event | category | flops | bytes accessed | tf_op | source)
XLA Modules:
  0.0 35.0 jit_solution(3589733996017285297)
XLA Ops:
  0.6 32.8 %shard_map.154 = (f32[16,1024]{1,0:T(8,128)S(1)}, f32[64,1024]{1,0:T(8,128)S(1)}, f32[64,1024]{1,0:T(8,128)S(1)}, f32[16,1024]{1,0:T(8,128)S(1)}, f32[64,1024]{1,0:T(8,128)S(1)}, /*index=5*/f32[64,1024]{1,0:T(8,128)S(1)}) custom-call(bf16[2048,1024]{1,0:T(8,128)(2,1)} %design_hbm.1, s32[4,1,512]{2,1,0:T(1,128)} %bitcast.3, s32[4,1,512]{2,1,0:T(1,128)} %bitcast.4, ...), custom_call_target="tpu_custom_call" | custom-call | tf_op jit(solution)/shard_map/pallas_call | solution.py:696
  33.4 1.6 %shard_map.155 = (f32[16,1024]{1,0:T(8,128)}, f32[16,64,64]{2,1,0:T(8,128)}, f32[16,64,64]{2,1,0:T(8,128)}, f32[16,1024]{1,0:T(8,128)}, f32[16,64,64]{2,1,0:T(8,128)}, /*index=5*/f32[16,64,64]{2,1,0:T(8,128)}) custom-call(f32[16,1024]{1,0:T(8,128)S(1)} %get-tuple-element.12.beta_n, f32[64,1024]{1,0:T(8,128)S(1)} %get-tuple-element.13.pools_n, ...), custom_call_target="tpu_custom_call" | custom-call | tf_op jit(solution)/shard_map/pallas_call | solution.py:754

commit v3 on v2

--- a/solution.py
+++ b/solution.py
@@ -27,14 +27,24 @@
 
 
 def code(x):
-    top = jnp.max(jnp.abs(x), axis=0, keepdims=True)
-    top = jnp.maximum(top, 1e-30)
-    q = jnp.round(x * (TOP / top)).astype(jnp.int32).astype(I16)
+    unit = min(128, x.shape[1])
+    pieces = [x[:, i : i + unit] for i in range(0, x.shape[1], unit)]
+    top = functools.reduce(jnp.maximum, [jnp.abs(p) for p in pieces])
+    top = jnp.maximum(jnp.max(top, axis=0, keepdims=True), 1e-30)
+    up = TOP / top
+    q = jnp.concatenate([jnp.round(p * up).astype(jnp.int32).astype(I16) for p in pieces], axis=1)
     return q, top * (1.0 / TOP)
 
 
 def decode(q, scale):
-    return q.astype(jnp.int32).astype(F32) * scale
+    unit = scale.shape[1]
+    return jnp.concatenate(
+        [
+            q[:, i : i + unit].astype(jnp.int32).astype(F32) * scale
+            for i in range(0, q.shape[1], unit)
+        ],
+        axis=1,
+    )
 
 
 def blocks_of(owned, g_own):
@@ -61,6 +71,11 @@
     beta_mn,
     pool_mn,
     region_mn,
+    pools_1,
+    regions_1,
+    pool_m1,
+    region_m1,
+    sums,
     design,
     labels,
     ids,
@@ -263,8 +278,6 @@
     n_cols = lanes // span
 
     def prologue():
-        fetch(0).wait()
-        lhs[pl.ds(0, chains), :] = beta[...].astype(BF16)
         lhs[pl.ds(chains, g_own), :] = (
             (
                 lax.broadcasted_iota(jnp.int32, (g_own, feats), 1)
@@ -282,6 +295,10 @@
             .astype(F32)
             .astype(BF16)
         )
+
+    def start_rows():
+        fetch(0).wait()
+        lhs[pl.ds(0, chains), :] = beta[...].astype(BF16)
         fetch(1).wait()
 
     def put_u4(c, blocks):
@@ -299,7 +316,7 @@
             put_u4(
                 c,
                 [
-                    pools_n[pl.ds(k * prow, prow), pl.ds(c * g_own, g_own)]
+                    pools_1[pl.ds(k * prow, prow), pl.ds(c * g_own, g_own)]
                     for k in range(nb)
                 ],
             )
@@ -314,22 +331,28 @@
 
     first = li * owned
 
-    def logits_first(k):
-        j = peer_of(k)
+    def sweep(k):
         fetch_rows(k).wait()
-        both = dot(lhs[...], design[j], NT)
-        local = ids[j] - first
-        block = local // prow
-        mask[j] = (
-            local - block * prow == lax.broadcasted_iota(jnp.int32, (prow, width), 0)
-        ).astype(F32)
-        slope = both[chains:]
-        for b in range(nb):
-            fold[j, pl.ds(b * g_own, g_own), :] = jnp.where(block == b, slope, 0.0).astype(BF16)
-        pool_term(j)
-        part[0, j] = term[j] + both[:chains]
-        if k:
-            rs_copy(0, k).start()
+        return dot(lhs[...], design[peer_of(k)], NT)
+
+    def logits_first():
+        both = sweep(order[0])
+        for i, k in enumerate(order):
+            ahead = sweep(order[i + 1]) if i + 1 < nf else None
+            j = peer_of(k)
+            local = ids[j] - first
+            block = local // prow
+            mask[j] = (
+                local - block * prow == lax.broadcasted_iota(jnp.int32, (prow, width), 0)
+            ).astype(F32)
+            slope = both[chains:]
+            for b in range(nb):
+                fold[j, pl.ds(b * g_own, g_own), :] = jnp.where(block == b, slope, 0.0).astype(BF16)
+            pool_term(j)
+            part[0, j] = term[j] + both[:chains]
+            if k:
+                rs_copy(0, k).start()
+            both = ahead
 
     def terms_next():
         for j in range(nf):
@@ -430,11 +453,11 @@
         rows = n_reg // nl
         for i in range(n_cols):
             hi, lo = halves(get(i))
-            s = dot(oht2, jnp.concatenate([hi, lo], axis=0))
-            for o in range(nl):
-                q, scale = code(s[o * rows : (o + 1) * rows])
-                part_q[t, o, :, cols(i)] = q
-                part_s[t, o, :, cols(i)] = scale
+            sums[:, :, cols(i)] = dot(oht2, jnp.concatenate([hi, lo], axis=0)).reshape(
+                nl, rows, span
+            )
+        for o in range(nl):
+            part_q[t, o], part_s[t, o] = code(sums[o])
 
     def region_send(t):
         for k in range(1, nl):
@@ -488,7 +511,7 @@
 
     def region_force(t, i, get_v, n):
         s = jnp.concatenate(
-            [decode(all_q[t, o, :, cols(i)], all_s[t, o, :, cols(i)]) for o in range(nl)], axis=0
+            [decode(all_q[t, o, :, cols(i)], all_s[t, o]) for o in range(nl)], axis=0
         )
         return PREC * (s - n * get_v(i))
 
@@ -501,8 +524,8 @@
         for i in range(n_cols):
             e = step_cols(i)
             m = wide(pool_m, i) + (0.5 * e) * (lik_cols(i) - dev[:, cols(i)])
-            pool_mn[:, cols(i)] = m
-            pools_n[:, cols(i)] = wide(pools, i) + e * m
+            pool_m1[:, cols(i)] = m
+            pools_1[:, cols(i)] = wide(pools, i) + e * m
 
     def region_next():
         fetch(8).wait()
@@ -514,20 +537,20 @@
             e = step_cols(i)
             g = region_force(0, i, lambda i: wide(regions, i), n)
             m = wide(region_m, i) + (0.5 * e) * g
-            region_mn[:, cols(i)] = m
-            regions_n[:, cols(i)] = wide(regions, i) + e * m
-        deviation(lambda i: pools_n[:, cols(i)], lambda i: regions_n[:, cols(i)])
+            region_m1[:, cols(i)] = m
+            regions_1[:, cols(i)] = wide(regions, i) + e * m
+        deviation(lambda i: pools_1[:, cols(i)], lambda i: regions_1[:, cols(i)])
 
     def region_last():
         region_gather(1)
         n = counts()
         for i in range(n_cols):
-            g = region_force(1, i, lambda i: regions_n[:, cols(i)], n)
-            region_mn[:, cols(i)] += (0.5 * step_cols(i)) * g
+            g = region_force(1, i, lambda i: regions_1[:, cols(i)], n)
+            region_m1[:, cols(i)] += (0.5 * step_cols(i)) * g
 
     def pool_last():
         for i in range(n_cols):
-            pool_mn[:, cols(i)] += (0.5 * step_cols(i)) * (lik_cols(i) - dev[:, cols(i)])
+            pool_m1[:, cols(i)] += (0.5 * step_cols(i)) * (lik_cols(i) - dev[:, cols(i)])
 
     def step_rows():
         chain = lax.broadcasted_iota(jnp.int32, (chains, 1), 0)
@@ -550,7 +573,7 @@
         pl.semaphore_wait(barrier, nf + nl - 2)
 
     def sum_next():
-        region_sum(1, lambda i: pools_n[:, cols(i)])
+        region_sum(1, lambda i: pools_1[:, cols(i)])
         region_send(1)
 
     def sent():
@@ -564,11 +587,15 @@
         for k in range(1, nl):
             pr_copy(k, li).wait_send()
 
+    def unpack(src, dst):
+        for c in range(chains):
+            dst[c] = src[:, pl.ds(c * g_own, g_own)]
+
     prologue()
+    start_rows()
     slopes_first()
     barrier_wait()
-    for k in order:
-        logits_first(k)
+    logits_first()
     region_first()
     deviation_first()
     wait_rest()
@@ -591,62 +618,35 @@
     region_reduce(0)
     beta_next()
     logits_next()
+    unpack(pools_1, pools_n)
     residuals(1)
     for k in arrive[:2]:
         population(1, k)
         likelihood(1, k)
-    region_next()
     region_reduce(1)
     for k in arrive[2:]:
         population(1, k)
     population_send(1)
     for k in arrive[2:]:
         likelihood(1, k)
+    region_next()
+    unpack(regions_1, regions_n)
     pool_last()
+    unpack(pool_m1, pool_mn)
     region_last()
+    unpack(region_m1, region_mn)
     beta_last()
     sent()
 
 
-def emit(
-    beta_n,
-    pools_n,
-    regions_n,
-    beta_mn,
-    pool_mn,
-    region_mn,
-    beta_o,
-    pools_o,
-    regions_o,
-    beta_mo,
-    pool_mo,
-    region_mo,
-    pools_v,
-    regions_v,
-    pool_mv,
-    region_mv,
-    sem,
-):
-    pending = [
-        pltpu.make_async_copy(beta_n, beta_o, sem.at[0]),
-        pltpu.make_async_copy(beta_mn, beta_mo, sem.at[1]),
+def emit(*refs):
+    n = len(refs) // 2
+    copies = [
+        pltpu.make_async_copy(refs[i], refs[n + i], refs[-1].at[i]) for i in range(n)
     ]
-    for copy in pending:
+    for copy in copies:
         copy.start()
-    wide = (
-        (pools_n, pools_v, pools_o),
-        (regions_n, regions_v, regions_o),
-        (pool_mn, pool_mv, pool_mo),
-        (region_mn, region_mv, region_mo),
-    )
-    for n, (src, tmp, dst) in enumerate(wide):
-        chains, _, g_own = tmp.shape
-        for c in range(chains):
-            tmp[c] = src[:, pl.ds(c * g_own, g_own)]
-        copy = pltpu.make_async_copy(tmp, dst, sem.at[2 + n])
-        copy.start()
-        pending.append(copy)
-    for copy in pending:
+    for copy in copies:
         copy.wait()
 
 
@@ -690,15 +690,17 @@
         region_momentum,
     )
     outs = (beta, pools, regions, beta_momentum, pool_momentum, region_momentum)
-    packed = tuple(
-        OUT(x.shape if x.ndim == 2 else (x.shape[1], lanes), F32) for x in outs
-    )
     results = pl.pallas_call(
         functools.partial(kernel, nf, nl),
-        out_shape=packed,
+        out_shape=tuple(pltpu.VMEM(x.shape, F32) for x in outs),
         in_specs=[hbm] * len(args),
         out_specs=tuple(vmem for _ in outs),
         scratch_shapes=[
+            pltpu.VMEM((owned, lanes), F32),
+            pltpu.VMEM((n_reg, lanes), F32),
+            pltpu.VMEM((owned, lanes), F32),
+            pltpu.VMEM((n_reg, lanes), F32),
+            pltpu.VMEM((nl, rows, lanes), F32),
             pltpu.VMEM((nf, width, feats), BF16),
             pltpu.VMEM((nf, 1, width), jnp.int32),
             pltpu.VMEM((nf, 1, width), jnp.int32),
@@ -723,13 +725,13 @@
             pltpu.VMEM((chains, width), F32),
             pltpu.VMEM((chains, feats), F32),
             pltpu.VMEM((2, nl, chains, feats), I16),
-            pltpu.VMEM((2, nl, 1, feats), F32),
+            pltpu.VMEM((2, nl, 1, min(128, feats)), F32),
             pltpu.VMEM((2, nl, rows, lanes), I16),
-            pltpu.VMEM((2, nl, 1, lanes), F32),
+            pltpu.VMEM((2, nl, 1, min(128, lanes)), F32),
             pltpu.VMEM((2, nl - 1, rows, lanes), I16),
-            pltpu.VMEM((2, nl - 1, 1, lanes), F32),
+            pltpu.VMEM((2, nl - 1, 1, min(128, lanes)), F32),
             pltpu.VMEM((2, nl, rows, lanes), I16),
-            pltpu.VMEM((2, nl, 1, lanes), F32),
+            pltpu.VMEM((2, nl, 1, min(128, lanes)), F32),
             pltpu.VMEM((nf, feats, width), BF16),
             pltpu.VMEM((min(256, feats),) * 2, BF16),
             dma((10,)),
@@ -756,19 +758,12 @@
         out_shape=tuple(jax.ShapeDtypeStruct(x.shape, x.dtype) for x in outs),
         in_specs=[vmem] * len(outs),
         out_specs=tuple(hbm for _ in outs),
-        scratch_shapes=[
-            pltpu.VMEM(pools.shape, F32),
-            pltpu.VMEM(regions.shape, F32),
-            pltpu.VMEM(pools.shape, F32),
-            pltpu.VMEM(regions.shape, F32),
-            dma((6,)),
-        ],
+        scratch_shapes=[dma((len(outs),))],
         compiler_params=pltpu.CompilerParams(vmem_limit_bytes=16 << 20),
     )(*results)
 
 
-VLIM = 24
-OUT = pltpu.VMEM
+VLIM = 30
 
 
 def solution(mesh):

time: 35.2 us -> 32.9 us (0.935)
  Pallas kernels: 34.4 us -> 32.1 us
    pallas_call x1, Pallas kernels: 32.8 us -> 30.7 us  [body(): pl.pallas_call(functools.partial(kernel, nf, nl), out_shape=tuple((pltpu....]
where the time goes in v3:
time: 32.9 us; the launch traced here: 32.8 us
  Pallas kernels  32.1 us (98%)
  between operations  0.64 us (2%)
    pallas_call x1, Pallas kernels, body(): pl.pallas_call(functools.partial(kernel, nf, nl), out_shape=tuple((pltpu....  30.7 us
    pallas_call x1, Pallas kernels, body(): pl.pallas_call(emit, out_shape=tuple((jax.ShapeDtypeStruct(x.shape, x.dty...  1.41 us

profile of v3, /device:TPU:0, one launch (start us, length us, event | category | flops | bytes accessed | tf_op | source)
XLA Modules:
  0.0 32.8 jit_solution(1640777592780258366)
XLA Ops:
  0.6 30.7 %shard_map.154 = (f32[16,1024]{1,0:T(8,128)S(1)}, f32[16,64,64]{2,1,0:T(8,128)S(1)}, f32[16,64,64]{2,1,0:T(8,128)S(1)}, f32[16,1024]{1,0:T(8,128)S(1)}, f32[16,6...) custom-call(bf16[2048,1024]{1,0:T(8,128)(2,1)} %design_hbm.1, s32[4,1,512]{2,1,0:T(1,128)} %bitcast.3, s32[4,1,512]{2,1,0:T(1,128)} %bitcast.4, ...), custom_call_target="tpu_custom_call" | custom-call | tf_op jit(solution)/shard_map/pallas_call | solution.py:693
  31.4 1.4 %shard_map.155 = (f32[16,1024]{1,0:T(8,128)}, f32[16,64,64]{2,1,0:T(8,128)}, f32[16,64,64]{2,1,0:T(8,128)}, f32[16,1024]{1,0:T(8,128)}, f32[16,64,64]{2,1,0:T(8,128)}, /*index=5*/f32[16,64,64]{2,1,0:T(8,128)}) custom-call(f32[16,1024]{1,0:T(8,128)S(1)} %get-tuple-element.12.refs_0_, f32[16,64,64]{2,1,0:T(8,128)S(1)} %get-tuple-element.13.refs_1_, ...), custom_call_target="tpu_custom_call" | custom-call | tf_op jit(solution)/shard_map/pallas_call | solution.py:756

commit v4 on v3

--- a/solution.py
+++ b/solution.py
@@ -34,6 +34,11 @@
     up = TOP / top
     q = jnp.concatenate([jnp.round(p * up).astype(jnp.int32).astype(I16) for p in pieces], axis=1)
     return q, top * (1.0 / TOP)
+
+
+def code_cols(x):
+    top = jnp.maximum(jnp.max(jnp.abs(x), axis=0, keepdims=True), 1e-30)
+    return jnp.round(x * (TOP / top)).astype(jnp.int32).astype(I16), top * (1.0 / TOP)
 
 
 def decode(q, scale):
@@ -95,8 +100,8 @@
     term,
     dev,
     part,
-    rs_buf,
-    resid,
+    line_q,
+    line_s,
     resid_f,
     xt_f,
     xt_q,
@@ -111,10 +116,8 @@
     eye,
     load,
     load_d,
-    s_rs,
-    r_rs,
-    s_ag,
-    r_ag,
+    s_lx,
+    r_lx,
     s_xt,
     r_xt,
     s_rr,
@@ -138,21 +141,27 @@
     side = max(1, 128 // g_own)
     span = side * g_own
     nx = nf // 2
-    order = [k for k in range(2, nf)] + [1, 0]
-    arrive = [0, 1] + [k for k in range(2, nf)]
 
     def peer_of(k):
         return lax.rem(fi // 2 + k // 2, nx) * 2 + lax.rem(fi + k, 2)
 
-    def source_of(k):
-        return lax.rem(fi // 2 + nx - k // 2, nx) * 2 + lax.rem(fi + k, 2)
-
-    def fetch_rows(k):
-        j = peer_of(k)
+    def each(n, act):
+        if n <= 4:
+            for k in range(n - 1, 0, -1):
+                act(k)
+        else:
+
+            def step(k, carry):
+                act(k)
+                return carry
+
+            lax.fori_loop(1, n, step, 0)
+
+    def fetch_rows(j):
         return pltpu.make_async_copy(
-            design_hbm.at[pl.ds(pl.multiple_of(j * width, width), width), :],
+            design_hbm.at[pl.ds(j * width, width), :],
             design.at[j],
-            load_d.at[k],
+            load_d.at[j],
         )
 
     def fetch(i):
@@ -170,24 +179,23 @@
         )[i]
         return pltpu.make_async_copy(src, dst, load.at[i])
 
-    for i in range(2):
-        fetch(i).start()
-    fetch_rows(order[0]).start()
-    fetch(2).start()
-    for k in order[1:]:
-        fetch_rows(k).start()
-    for i in range(3, 10):
-        fetch(i).start()
-
     barrier = pltpu.get_barrier_semaphore()
-    for k in range(1, nf):
-        pl.semaphore_signal(
-            barrier, inc=1, device_id={"feat": peer_of(k)}, device_id_type=MESH
-        )
-    for k in range(1, nl):
+    for k in range(nl - 1, 0, -1):
         pl.semaphore_signal(
             barrier, inc=1, device_id={"loan": lax.rem(li + k, nl)}, device_id_type=MESH
         )
+    each(
+        nf,
+        lambda k: pl.semaphore_signal(
+            barrier, inc=1, device_id={"feat": peer_of(k)}, device_id_type=MESH
+        ),
+    )
+
+    for i in range(2):
+        fetch(i).start()
+    fetch_rows(0).start()
+    fetch(2).start()
+    fetch_rows(1).start()
 
     def remote(src, dst, ss, rs, axis, peer):
         return pltpu.make_async_remote_copy(
@@ -199,35 +207,52 @@
             device_id_type=MESH,
         )
 
-    def rs_copy(t, k):
-        peer = peer_of(k)
-        return remote(
-            part.at[t, peer], rs_buf.at[t, k - 1], s_rs.at[t, k - 1], r_rs.at[t, k - 1], "feat", peer
-        )
-
-    def ag_copy(t, k, slot):
-        return remote(
-            resid.at[t, slot],
-            resid.at[t, slot],
-            s_ag.at[t, k - 1],
-            r_ag.at[t, k - 1],
-            "feat",
-            peer_of(k),
-        )
+    batch = (1, 2 - nf % 2)
+
+    def line_copies(t, k, j):
+        some = pl.ds(j, batch[t])
+        return [
+            remote(
+                ref.at[t, 0, some],
+                ref.at[t, k, some],
+                s_lx.at[i],
+                r_lx.at[i, t, j],
+                "feat",
+                peer_of(k),
+            )
+            for i, ref in enumerate((line_s, line_q))
+        ]
+
+    def line_send(t, j, x):
+        part[t, j] = x
+        line_q[t, 0, j], line_s[t, 0, j] = code_cols(x)
+        if t == 0 and j == 0:
+            pl.semaphore_wait(barrier, nf + nl - 2)
+
+        last = j - batch[t] + 1
+
+        def go(k):
+            for copy in line_copies(t, k, last):
+                copy.start()
+
+        if last % batch[t] == 0:
+            each(nf, go)
+
+    def settle(view, sem):
+        pltpu.make_async_copy(view, view, sem).wait()
+
+    others_f, others_l = pl.ds(1, nf - 1), pl.ds(1, nl - 1)
 
     def loan_peer(k):
         return lax.rem(li + k, nl)
-
-    def loan_source(k):
-        return lax.rem(li + nl - k, nl)
 
     def xt_copies(t, k):
         return [
             remote(
                 ref.at[t, 0],
                 ref.at[t, k],
-                s_xt.at[i, t, k - 1],
-                r_xt.at[i, t, k - 1],
+                s_xt.at[i],
+                r_xt.at[i, t],
                 "loan",
                 loan_peer(k),
             )
@@ -240,8 +265,8 @@
             remote(
                 src.at[t, peer],
                 dst.at[t, k - 1],
-                s_rr.at[i, t, k - 1],
-                r_rr.at[i, t, k - 1],
+                s_rr.at[i],
+                r_rr.at[i, t],
                 "loan",
                 peer,
             )
@@ -253,8 +278,8 @@
             remote(
                 ref.at[t, owner],
                 ref.at[t, owner],
-                s_ra.at[i, t, k - 1],
-                r_ra.at[i, t, k - 1],
+                s_ra.at[i],
+                r_ra.at[i, t],
                 "loan",
                 loan_peer(k),
             )
@@ -263,7 +288,7 @@
 
     def pr_copy(k, owner):
         return remote(
-            pri.at[owner], pri.at[owner], s_pr.at[k - 1], r_pr.at[k - 1], "loan", loan_peer(k)
+            pri.at[owner], pri.at[owner], s_pr, r_pr, "loan", loan_peer(k)
         )
 
     def onehot_t(row):
@@ -278,15 +303,18 @@
     n_cols = lanes // span
 
     def prologue():
-        lhs[pl.ds(chains, g_own), :] = (
+        size = eye.shape[0]
+        tile = size // stride
+        pick = (
             (
-                lax.broadcasted_iota(jnp.int32, (g_own, feats), 1)
-                == stride * lax.broadcasted_iota(jnp.int32, (g_own, feats), 0)
+                lax.broadcasted_iota(jnp.int32, (tile, size), 1)
+                == stride * lax.broadcasted_iota(jnp.int32, (tile, size), 0)
             )
             .astype(F32)
             .astype(BF16)
         )
-        size = eye.shape[0]
+        for i in range(feats // size):
+            lhs[pl.ds(chains, tile), pl.ds(i * size, size)] = pick
         eye[...] = (
             (
                 lax.broadcasted_iota(jnp.int32, (size, size), 0)
@@ -298,6 +326,8 @@
 
     def start_rows():
         fetch(0).wait()
+        for j in range(2, nf):
+            fetch_rows(j).start()
         lhs[pl.ds(0, chains), :] = beta[...].astype(BF16)
         fetch(1).wait()
 
@@ -331,69 +361,91 @@
 
     first = li * owned
 
-    def sweep(k):
-        fetch_rows(k).wait()
-        return dot(lhs[...], design[peer_of(k)], NT)
+    turned = 2
+
+    def sweep(j):
+        fetch_rows(j).wait()
+        size = eye.shape[0]
+        line, slope = None, []
+        for i in range(feats // size):
+            if i < turned:
+                y = design[j, :, pl.ds(i * size, size)].T
+                flipped[j, pl.ds(i * size, size), :] = y
+                x = dot(lhs[:, pl.ds(i * size, size)], y)
+            else:
+                x = dot(lhs[:, pl.ds(i * size, size)], design[j, :, pl.ds(i * size, size)], NT)
+            line = x[:chains] if line is None else line + x[:chains]
+            slope.append(x[chains:])
+        return line, jnp.concatenate(slope, axis=0)
 
     def logits_first():
-        both = sweep(order[0])
-        for i, k in enumerate(order):
-            ahead = sweep(order[i + 1]) if i + 1 < nf else None
-            j = peer_of(k)
+        both = sweep(0)
+        for j in range(nf):
+            ahead = sweep(j + 1) if j + 1 < nf else None
             local = ids[j] - first
             block = local // prow
             mask[j] = (
                 local - block * prow == lax.broadcasted_iota(jnp.int32, (prow, width), 0)
             ).astype(F32)
-            slope = both[chains:]
+            line, slope = both
             for b in range(nb):
                 fold[j, pl.ds(b * g_own, g_own), :] = jnp.where(block == b, slope, 0.0).astype(BF16)
             pool_term(j)
-            part[0, j] = term[j] + both[:chains]
-            if k:
-                rs_copy(0, k).start()
+            line_send(0, j, term[j] + line)
+            if j == 0:
+                for i in range(3, 10):
+                    fetch(i).start()
             both = ahead
 
     def terms_next():
         for j in range(nf):
             pool_term(j)
 
-    def flip(k):
-        j = peer_of(k)
+    def flip(j):
         size = eye.shape[0]
-        for i in range(feats // size):
+        for i in range(turned, feats // size):
             x = dot(eye[...], design[j, :, pl.ds(i * size, size)], NT)
             flipped[j, pl.ds(i * size, size), :] = x.astype(BF16)
 
     def logits_next():
         b16 = beta_n[...].astype(BF16)
-        for k in order:
-            j = peer_of(k)
-            part[1, j] = term[j] + dot(b16, flipped[j])
-            if k:
-                rs_copy(1, k).start()
-
-    def residuals(t):
-        logit = part[t, fi]
-        for k in range(1, nf):
-            rs_copy(t, k).wait_recv()
-            logit = logit + rs_buf[t, k - 1]
-        mine = (labels[fi].astype(F32) - jax.nn.sigmoid(logit)).astype(BF16)
-        resid[t, fi] = mine
-        for k in order[:-1]:
-            ag_copy(t, k, fi).start()
-
-    def population(t, k):
-        s = source_of(k)
-        if k:
-            ag_copy(t, k, s).wait_recv()
-        x = dot(resid[t, s], design[s])
-        if k == arrive[0]:
+        for j in range(nf):
+            line_send(1, j, term[j] + dot(b16, flipped[j]))
+
+    def residual(t, j):
+        if j % batch[t] == 0:
+            some = pl.ds(j, batch[t])
+            settle(line_s.at[t, others_f, some], r_lx.at[0, t, j])
+            settle(line_q.at[t, others_f, some], r_lx.at[1, t, j])
+
+        def add(k, logit):
+            return logit + line_q[t, k, j].astype(jnp.int32).astype(F32) * line_s[t, k, j]
+
+        logit = part[t, j]
+        if nf <= 4:
+            for k in range(1, nf):
+                logit = add(k, logit)
+        else:
+            logit = lax.fori_loop(1, nf, add, logit)
+        mine = (labels[j].astype(F32) - jax.nn.sigmoid(logit)).astype(BF16)
+        resid_f[j] = mine.astype(F32)
+        return mine
+
+    def residuals(t, j):
+        x = dot(residual(t, j), design[j])
+        if j == 0:
             xt_f[...] = x
-        elif k != arrive[-1]:
+        elif j != nf - 1:
             xt_f[...] += x
         else:
             xt_q[t, 0], xt_s[t, 0] = code(xt_f[...] + x)
+
+    def residuals_all(t):
+        mine = [residual(t, j) for j in range(nf)]
+        x = dot(mine[0], design[0])
+        for j in range(1, nf):
+            x = x + dot(mine[j], design[j])
+        xt_q[t, 0], xt_s[t, 0] = code(x)
 
     def population_send(t):
         for k in range(1, nl):
@@ -401,24 +453,21 @@
                 copy.start()
 
     def population_sum(t):
-        for k in range(1, nl):
-            for copy in xt_copies(t, k):
-                copy.wait_recv()
+        settle(xt_s.at[t, others_l], r_xt.at[0, t])
+        settle(xt_q.at[t, others_l], r_xt.at[1, t])
         total = decode(xt_q[t, li], xt_s[t, li])
         for j in range(1, nl):
             slot = lax.rem(li + nl - j, nl)
             total = total + decode(xt_q[t, slot], xt_s[t, slot])
         return total
 
-    def likelihood(t, k):
-        s = source_of(k)
-        resid_f[...] = resid[t, s].astype(F32)
-        m = mask[s]
+    def likelihood(j):
+        m = mask[j]
         a = jnp.concatenate(
-            [(resid_f[pl.ds(c, 1), :] * m).astype(BF16) for c in range(chains)], axis=0
+            [(resid_f[j, pl.ds(c, 1), :] * m).astype(BF16) for c in range(chains)], axis=0
         )
-        x = dot(a, fold[s], NT)
-        if k == arrive[0]:
+        x = dot(a, fold[j], NT)
+        if j == 0:
             lik[...] = x
         else:
             lik[...] += x
@@ -488,10 +537,10 @@
         deviation(lambda i: wide(pools, i), lambda i: wide(regions, i))
 
     def region_reduce(t):
+        settle(buf_s.at[t], r_rr.at[0, t])
+        settle(buf_q.at[t], r_rr.at[1, t])
         total = decode(part_q[t, li], part_s[t, li])
         for k in range(1, nl):
-            for copy in rr_copies(t, k):
-                copy.wait_recv()
             total = total + decode(buf_q[t, k - 1], buf_s[t, k - 1])
         all_q[t, li], all_s[t, li] = code(total)
         for k in range(1, nl):
@@ -499,9 +548,8 @@
                 copy.start()
 
     def region_gather(t):
-        for k in range(1, nl):
-            for copy in ra_copies(t, k, loan_source(k)):
-                copy.wait_recv()
+        settle(all_s.at[t, others_l], r_ra.at[0, t])
+        settle(all_q.at[t, others_l], r_ra.at[1, t])
 
     def counts():
         n = jnp.zeros((n_reg, 1), F32)
@@ -530,8 +578,7 @@
     def region_next():
         fetch(8).wait()
         region_gather(0)
-        for k in range(1, nl):
-            pr_copy(k, loan_source(k)).wait_recv()
+        settle(pri.at[others_l], r_pr)
         n = counts()
         for i in range(n_cols):
             e = step_cols(i)
@@ -569,23 +616,20 @@
     def beta_last():
         beta_mn[...] += (0.5 * step_rows()) * (population_sum(1) - total_feats * beta_n[...])
 
-    def barrier_wait():
-        pl.semaphore_wait(barrier, nf + nl - 2)
-
     def sum_next():
         region_sum(1, lambda i: pools_1[:, cols(i)])
         region_send(1)
 
     def sent():
-        for t in range(2):
-            for k in range(1, nf):
-                rs_copy(t, k).wait_send()
-                ag_copy(t, k, fi).wait_send()
-            for k in range(1, nl):
-                for copy in xt_copies(t, k) + rr_copies(t, k) + ra_copies(t, k, li):
-                    copy.wait_send()
-        for k in range(1, nl):
-            pr_copy(k, li).wait_send()
+        settle(line_s.at[:, others_f], s_lx.at[0])
+        settle(line_q.at[:, others_f], s_lx.at[1])
+        settle(xt_s.at[:, others_l], s_xt.at[0])
+        settle(xt_q.at[:, others_l], s_xt.at[1])
+        settle(buf_s, s_rr.at[0])
+        settle(buf_q, s_rr.at[1])
+        settle(all_s.at[:, others_l], s_ra.at[0])
+        settle(all_q.at[:, others_l], s_ra.at[1])
+        settle(pri.at[others_l], s_pr)
 
     def unpack(src, dst):
         for c in range(chains):
@@ -594,41 +638,31 @@
     prologue()
     start_rows()
     slopes_first()
-    barrier_wait()
     logits_first()
     region_first()
     deviation_first()
     wait_rest()
-    residuals(0)
-    for k in arrive[:2]:
-        population(0, k)
-        likelihood(0, k)
-    flip(arrive[0])
-    for k in arrive[2:]:
-        population(0, k)
+    for j in range(nf - 1):
+        residuals(0, j)
+        likelihood(j)
+    residuals(0, nf - 1)
     population_send(0)
-    for k in arrive[2:]:
-        likelihood(0, k)
+    likelihood(nf - 1)
     pool_update()
     slopes_next()
     terms_next()
     sum_next()
-    for k in arrive[1:]:
-        flip(k)
-    region_reduce(0)
+    for j in range(nf):
+        flip(j)
     beta_next()
     logits_next()
+    region_reduce(0)
     unpack(pools_1, pools_n)
-    residuals(1)
-    for k in arrive[:2]:
-        population(1, k)
-        likelihood(1, k)
     region_reduce(1)
-    for k in arrive[2:]:
-        population(1, k)
+    residuals_all(1)
     population_send(1)
-    for k in arrive[2:]:
-        likelihood(1, k)
+    for j in range(nf):
+        likelihood(j)
     region_next()
     unpack(regions_1, regions_n)
     pool_last()
@@ -712,7 +746,7 @@
             pltpu.VMEM(beta.shape, F32),
             pltpu.VMEM(pools.shape, F32),
             pltpu.VMEM(regions.shape, F32),
-            pltpu.VMEM((chains + g_own, feats), BF16),
+            pltpu.VMEM((chains + g_own * min(256, feats) // feats, feats), BF16),
             pltpu.VMEM((nf, prow, width), F32),
             pltpu.VMEM((nf, nb * g_own, width), BF16),
             pltpu.VMEM((2 * chains * prow, nb * g_own), BF16),
@@ -720,9 +754,9 @@
             pltpu.VMEM((nf, chains, width), F32),
             pltpu.VMEM((owned, lanes), F32),
             pltpu.VMEM((2, nf, chains, width), F32),
-            pltpu.VMEM((2, nf - 1, chains, width), F32),
-            pltpu.VMEM((2, nf, chains, width), BF16),
-            pltpu.VMEM((chains, width), F32),
+            pltpu.VMEM((2, nf, nf, chains, width), I16),
+            pltpu.VMEM((2, nf, nf, 1, width), F32),
+            pltpu.VMEM((nf, chains, width), F32),
             pltpu.VMEM((chains, feats), F32),
             pltpu.VMEM((2, nl, chains, feats), I16),
             pltpu.VMEM((2, nl, 1, min(128, feats)), F32),
@@ -736,18 +770,16 @@
             pltpu.VMEM((min(256, feats),) * 2, BF16),
             dma((10,)),
             dma((nf,)),
-            dma((2, nf - 1)),
-            dma((2, nf - 1)),
-            dma((2, nf - 1)),
-            dma((2, nf - 1)),
-            dma((2, 2, nl - 1)),
-            dma((2, 2, nl - 1)),
-            dma((2, 2, nl - 1)),
-            dma((2, 2, nl - 1)),
-            dma((2, 2, nl - 1)),
-            dma((2, 2, nl - 1)),
-            dma((nl - 1,)),
-            dma((nl - 1,)),
+            dma((2,)),
+            dma((2, 2, nf)),
+            dma((2,)),
+            dma((2, 2)),
+            dma((2,)),
+            dma((2, 2)),
+            dma((2,)),
+            dma((2, 2)),
+            dma,
+            dma,
         ],
         compiler_params=pltpu.CompilerParams(
             collective_id=0, has_side_effects=True, vmem_limit_bytes=VLIM << 20

time: 32.9 us -> 30.2 us (0.918)
  Pallas kernels: 32.1 us -> 29.4 us
    pallas_call x1, Pallas kernels: 30.7 us -> 28 us  [body(): pl.pallas_call(functools.partial(kernel, nf, nl), out_shape=tuple((pltpu....]
where the time goes in v4:
time: 30.2 us; the launch traced here: 30.1 us
  Pallas kernels  29.4 us (97%)
  between operations  0.64 us (2%)
    pallas_call x1, Pallas kernels, body(): pl.pallas_call(functools.partial(kernel, nf, nl), out_shape=tuple((pltpu....  28 us
    pallas_call x1, Pallas kernels, body(): pl.pallas_call(emit, out_shape=tuple((jax.ShapeDtypeStruct(x.shape, x.dty...  1.41 us

profile of v4, /device:TPU:0, one launch (start us, length us, event | category | flops | bytes accessed | tf_op | source)
XLA Modules:
  0.0 30.1 jit_solution(2472336422868668007)
XLA Ops:
  0.6 28.0 %shard_map.154 = (f32[16,1024]{1,0:T(8,128)S(1)}, f32[16,64,64]{2,1,0:T(8,128)S(1)}, f32[16,64,64]{2,1,0:T(8,128)S(1)}, f32[16,1024]{1,0:T(8,128)S(1)}, f32[16,6...) custom-call(bf16[2048,1024]{1,0:T(8,128)(2,1)} %design_hbm.1, s32[4,1,512]{2,1,0:T(1,128)} %bitcast.3, s32[4,1,512]{2,1,0:T(1,128)} %bitcast.4, ...), custom_call_target="tpu_custom_call" | custom-call | tf_op jit(solution)/shard_map/pallas_call | solution.py:727
  28.7 1.4 %shard_map.155 = (f32[16,1024]{1,0:T(8,128)}, f32[16,64,64]{2,1,0:T(8,128)}, f32[16,64,64]{2,1,0:T(8,128)}, f32[16,1024]{1,0:T(8,128)}, f32[16,64,64]{2,1,0:T(8,128)}, /*index=5*/f32[16,64,64]{2,1,0:T(8,128)}) custom-call(f32[16,1024]{1,0:T(8,128)S(1)} %get-tuple-element.12.refs_0_, f32[16,64,64]{2,1,0:T(8,128)S(1)} %get-tuple-element.13.refs_1_, ...), custom_call_target="tpu_custom_call" | custom-call | tf_op jit(solution)/shard_map/pallas_call | solution.py:788

commit v5 on v4

--- a/solution.py
+++ b/solution.py
@@ -243,18 +243,25 @@
 
     others_f, others_l = pl.ds(1, nf - 1), pl.ds(1, nl - 1)
 
-    def loan_peer(k):
-        return lax.rem(li + k, nl)
+    def loan_peer(i):
+        right = li // ((nl + 1) // 2)
+        place = li * (1 - right) + (nl - 1 - li) * right
+        far = nl - 1 - i - (place + 1 + i) // nl
+        return far * (1 - right) + (nl - 1 - far) * right
+
+    def loan_slot(peer):
+        return lax.rem(peer - li + nl, nl)
 
     def xt_copies(t, k):
+        peer = loan_peer(k)
         return [
             remote(
                 ref.at[t, 0],
-                ref.at[t, k],
+                ref.at[t, loan_slot(peer)],
                 s_xt.at[i],
                 r_xt.at[i, t],
                 "loan",
-                loan_peer(k),
+                peer,
             )
             for i, ref in enumerate((xt_s, xt_q))
         ]
@@ -264,7 +271,7 @@
         return [
             remote(
                 src.at[t, peer],
-                dst.at[t, k - 1],
+                dst.at[t, loan_slot(peer) - 1],
                 s_rr.at[i],
                 r_rr.at[i, t],
                 "loan",
@@ -368,34 +375,34 @@
         size = eye.shape[0]
         line, slope = None, []
         for i in range(feats // size):
-            if i < turned:
-                y = design[j, :, pl.ds(i * size, size)].T
-                flipped[j, pl.ds(i * size, size), :] = y
-                x = dot(lhs[:, pl.ds(i * size, size)], y)
+            depth = pl.ds(i * size, size)
+            if i % 2 == 1 and i // 2 < turned or i == 0 and turned > 2:
+                flipped[j, depth, :] = design[j, :, depth].T
+                x = dot(lhs[:, depth], flipped[j, depth, :])
             else:
-                x = dot(lhs[:, pl.ds(i * size, size)], design[j, :, pl.ds(i * size, size)], NT)
+                x = dot(lhs[:, depth], design[j, :, depth], NT)
             line = x[:chains] if line is None else line + x[:chains]
             slope.append(x[chains:])
-        return line, jnp.concatenate(slope, axis=0)
+        local = ids[j] - first
+        block = local // prow
+        mask[j] = (
+            local - block * prow == lax.broadcasted_iota(jnp.int32, (prow, width), 0)
+        ).astype(F32)
+        slope = jnp.concatenate(slope, axis=0)
+        for b in range(nb):
+            fold[j, pl.ds(b * g_own, g_own), :] = jnp.where(block == b, slope, 0.0).astype(BF16)
+        part[0, j] = line
 
     def logits_first():
-        both = sweep(0)
+        sweep(0)
         for j in range(nf):
-            ahead = sweep(j + 1) if j + 1 < nf else None
-            local = ids[j] - first
-            block = local // prow
-            mask[j] = (
-                local - block * prow == lax.broadcasted_iota(jnp.int32, (prow, width), 0)
-            ).astype(F32)
-            line, slope = both
-            for b in range(nb):
-                fold[j, pl.ds(b * g_own, g_own), :] = jnp.where(block == b, slope, 0.0).astype(BF16)
+            if j + 1 < nf:
+                sweep(j + 1)
             pool_term(j)
-            line_send(0, j, term[j] + line)
+            line_send(0, j, term[j] + part[0, j])
             if j == 0:
-                for i in range(3, 10):
+                for i in (3, 4, 5, 6, 7, 8, 9):
                     fetch(i).start()
-            both = ahead
 
     def terms_next():
         for j in range(nf):
@@ -403,7 +410,9 @@
 
     def flip(j):
         size = eye.shape[0]
-        for i in range(turned, feats // size):
+        for i in range(feats // size):
+            if i % 2 == 1 and i // 2 < turned or i == 0 and turned > 2:
+                continue
             x = dot(eye[...], design[j, :, pl.ds(i * size, size)], NT)
             flipped[j, pl.ds(i * size, size), :] = x.astype(BF16)
 
@@ -448,7 +457,7 @@
         xt_q[t, 0], xt_s[t, 0] = code(x)
 
     def population_send(t):
-        for k in range(1, nl):
+        for k in range(nl - 1):
             for copy in xt_copies(t, k):
                 copy.start()
 
@@ -509,7 +518,7 @@
             part_q[t, o], part_s[t, o] = code(sums[o])
 
     def region_send(t):
-        for k in range(1, nl):
+        for k in range(nl - 1):
             for copy in rr_copies(t, k):
                 copy.start()
 
@@ -528,7 +537,7 @@
     def region_first():
         fetch(4).wait()
         region_sum(0, lambda i: wide(pools, i))
-        for k in range(1, nl):
+        for k in range(nl - 1):
             pr_copy(k, li).start()
         region_send(0)
 
@@ -543,7 +552,7 @@
         for k in range(1, nl):
             total = total + decode(buf_q[t, k - 1], buf_s[t, k - 1])
         all_q[t, li], all_s[t, li] = code(total)
-        for k in range(1, nl):
+        for k in range(nl - 1):
             for copy in ra_copies(t, k, li):
                 copy.start()
 

time: 30.2 us -> 30 us (level)
  no operation moved by 1% of the time
where the time goes in v5:
time: 30 us; the launch traced here: 29.8 us
  Pallas kernels  29.2 us (97%)
  between operations  0.64 us (2%)
    pallas_call x1, Pallas kernels, body(): pl.pallas_call(functools.partial(kernel, nf, nl), out_shape=tuple((pltpu....  27.8 us
    pallas_call x1, Pallas kernels, body(): pl.pallas_call(emit, out_shape=tuple((jax.ShapeDtypeStruct(x.shape, x.dty...  1.41 us

profile of v5, /device:TPU:0, one launch (start us, length us, event | category | flops | bytes accessed | tf_op | source)
XLA Modules:
  0.0 29.8 jit_solution(10891708114910677301)
XLA Ops:
  0.6 27.8 %shard_map.154 = (f32[16,1024]{1,0:T(8,128)S(1)}, f32[16,64,64]{2,1,0:T(8,128)S(1)}, f32[16,64,64]{2,1,0:T(8,128)S(1)}, f32[16,1024]{1,0:T(8,128)S(1)}, f32[16,6...) custom-call(bf16[2048,1024]{1,0:T(8,128)(2,1)} %design_hbm.1, s32[4,1,512]{2,1,0:T(1,128)} %bitcast.3, s32[4,1,512]{2,1,0:T(1,128)} %bitcast.4, ...), custom_call_target="tpu_custom_call" | custom-call | tf_op jit(solution)/shard_map/pallas_call | solution.py:736
  28.4 1.4 %shard_map.155 = (f32[16,1024]{1,0:T(8,128)}, f32[16,64,64]{2,1,0:T(8,128)}, f32[16,64,64]{2,1,0:T(8,128)}, f32[16,1024]{1,0:T(8,128)}, f32[16,64,64]{2,1,0:T(8,128)}, /*index=5*/f32[16,64,64]{2,1,0:T(8,128)}) custom-call(f32[16,1024]{1,0:T(8,128)S(1)} %get-tuple-element.12.refs_0_, f32[16,64,64]{2,1,0:T(8,128)S(1)} %get-tuple-element.13.refs_1_, ...), custom_call_target="tpu_custom_call" | custom-call | tf_op jit(solution)/shard_map/pallas_call | solution.py:797

commit v6 on v5

--- a/solution.py
+++ b/solution.py
@@ -207,7 +207,7 @@
             device_id_type=MESH,
         )
 
-    batch = (1, 2 - nf % 2)
+    batch = (1, 1)
 
     def line_copies(t, k, j):
         some = pl.ds(j, batch[t])
@@ -450,11 +450,18 @@
             xt_q[t, 0], xt_s[t, 0] = code(xt_f[...] + x)
 
     def residuals_all(t):
-        mine = [residual(t, j) for j in range(nf)]
-        x = dot(mine[0], design[0])
-        for j in range(1, nf):
-            x = x + dot(mine[j], design[j])
-        xt_q[t, 0], xt_s[t, 0] = code(x)
+        half = batch[t]
+        for i in range(0, nf, half):
+            mine = [residual(t, j) for j in range(i, i + half)]
+            x = dot(mine[0], design[i])
+            for j in range(1, half):
+                x = x + dot(mine[j], design[i + j])
+            if i == 0:
+                xt_f[...] = x
+            elif i + half < nf:
+                xt_f[...] += x
+            else:
+                xt_q[t, 0], xt_s[t, 0] = code(xt_f[...] + x)
 
     def population_send(t):
         for k in range(nl - 1):
@@ -663,9 +670,9 @@
     sum_next()
     for j in range(nf):
         flip(j)
+    region_reduce(0)
     beta_next()
     logits_next()
-    region_reduce(0)
     unpack(pools_1, pools_n)
     region_reduce(1)
     residuals_all(1)

time: 30 us -> 30 us (level)
  no operation moved by 1% of the time
where the time goes in v6:
time: 30 us; the launch traced here: 29.8 us
  Pallas kernels  29.2 us (97%)
  between operations  0.64 us (2%)
    pallas_call x1, Pallas kernels, body(): pl.pallas_call(functools.partial(kernel, nf, nl), out_shape=tuple((pltpu....  27.8 us
    pallas_call x1, Pallas kernels, body(): pl.pallas_call(emit, out_shape=tuple((jax.ShapeDtypeStruct(x.shape, x.dty...  1.41 us

profile of v6, /device:TPU:0, one launch (start us, length us, event | category | flops | bytes accessed | tf_op | source)
XLA Modules:
  0.0 29.8 jit_solution(14152792953221933326)
XLA Ops:
  0.6 27.8 %shard_map.154 = (f32[16,1024]{1,0:T(8,128)S(1)}, f32[16,64,64]{2,1,0:T(8,128)S(1)}, f32[16,64,64]{2,1,0:T(8,128)S(1)}, f32[16,1024]{1,0:T(8,128)S(1)}, f32[16,6...) custom-call(bf16[2048,1024]{1,0:T(8,128)(2,1)} %design_hbm.1, s32[4,1,512]{2,1,0:T(1,128)} %bitcast.3, s32[4,1,512]{2,1,0:T(1,128)} %bitcast.4, ...), custom_call_target="tpu_custom_call" | custom-call | tf_op jit(solution)/shard_map/pallas_call | solution.py:743
  28.4 1.4 %shard_map.155 = (f32[16,1024]{1,0:T(8,128)}, f32[16,64,64]{2,1,0:T(8,128)}, f32[16,64,64]{2,1,0:T(8,128)}, f32[16,1024]{1,0:T(8,128)}, f32[16,64,64]{2,1,0:T(8,128)}, /*index=5*/f32[16,64,64]{2,1,0:T(8,128)}) custom-call(f32[16,1024]{1,0:T(8,128)S(1)} %get-tuple-element.12.refs_0_, f32[16,64,64]{2,1,0:T(8,128)S(1)} %get-tuple-element.13.refs_1_, ...), custom_call_target="tpu_custom_call" | custom-call | tf_op jit(solution)/shard_map/pallas_call | solution.py:804
